TPU v7x, 32 devices: a whole 2x2x4 slice. The times are simulated.
32 devices in a mesh: wshard: 4 (over y, x), seq: 8 (over z, core).
Axes of the slice: x: 2, y: 2, z: 4, core: 2. Of those that a mesh axis runs over, the one named last changes fastest.
Arguments:
- block_input: bfloat16 [8, 1024, 1536], P('wshard', 'seq'), may hold values from -6 to 6
- cotangent: bfloat16 [8, 1024, 1536], P('wshard', 'seq'), may hold values from -6 to 6
- norm_gain: bfloat16 [1536], P('wshard'), may hold values from 0.5 to 1.5
- norm_mean: float32 [1536], P(('wshard', 'seq')), may hold values from -16 to 16
- norm_square: float32 [1536], P(('wshard', 'seq')), may hold values from 0.16384 to 1.6384
- inproj_weight: bfloat16 [1536, 6448], P('wshard'), may hold values from -0.15625 to 0.15625
- inproj_mean: float32 [1536, 6448], P(('wshard', 'seq')), may hold values from -16 to 16
- inproj_square: float32 [1536, 6448], P(('wshard', 'seq')), may hold values from 0.16384 to 1.6384
- conv_params: bfloat16 [5, 3328], P(None, 'wshard'), may hold values from -0.5 to 0.5
- conv_mean: float32 [5, 3328], P(None, ('wshard', 'seq')), may hold values from -16 to 16
- conv_square: float32 [5, 3328], P(None, ('wshard', 'seq')), may hold values from 0.16384 to 1.6384
- head_params: bfloat16 [3, 48], P(None, 'wshard'), may hold values from -7 to 2.8, as said below
- head_mean: float32 [3, 48], P(None, 'wshard'), may hold values from -16 to 16
- head_square: float32 [3, 48], P(None, 'wshard'), may hold values from 0.16384 to 1.6384
- gate_gain: bfloat16 [3072], P('wshard'), may hold values from 0.5 to 1.5
- gate_mean: float32 [3072], P(('wshard', 'seq')), may hold values from -16 to 16
- gate_square: float32 [3072], P(('wshard', 'seq')), may hold values from 0.16384 to 1.6384
- outproj_weight: bfloat16 [3072, 1536], P('wshard'), may hold values from -0.109375 to 0.109375
- outproj_mean: float32 [3072, 1536], P(('wshard', 'seq')), may hold values from -16 to 16
- outproj_square: float32 [3072, 1536], P(('wshard', 'seq')), may hold values from 0.16384 to 1.6384
Outputs:
- block_output: float32 [8, 1024, 1536], P('wshard', 'seq')
- input_grad: float32 [8, 1024, 1536], P('wshard', 'seq')
- norm_grad: float32 [1536], P(('wshard', 'seq'))
- norm_newmean: float32 [1536], P(('wshard', 'seq'))
- norm_newsquare: float32 [1536], P(('wshard', 'seq'))
- norm_update: float32 [1536], P(('wshard', 'seq'))
- inproj_grad: float32 [1536, 6448], P(('wshard', 'seq'))
- inproj_newmean: float32 [1536, 6448], P(('wshard', 'seq'))
- inproj_newsquare: float32 [1536, 6448], P(('wshard', 'seq'))
- inproj_update: float32 [1536, 6448], P(('wshard', 'seq'))
- conv_grad: float32 [5, 3328], P(None, ('wshard', 'seq'))
- conv_newmean: float32 [5, 3328], P(None, ('wshard', 'seq'))
- conv_newsquare: float32 [5, 3328], P(None, ('wshard', 'seq'))
- conv_update: float32 [5, 3328], P(None, ('wshard', 'seq'))
- head_grad: float32 [3, 48], P(None, 'wshard')
- head_newmean: float32 [3, 48], P(None, 'wshard')
- head_newsquare: float32 [3, 48], P(None, 'wshard')
- head_update: float32 [3, 48], P(None, 'wshard')
- gate_grad: float32 [3072], P(('wshard', 'seq'))
- gate_newmean: float32 [3072], P(('wshard', 'seq'))
- gate_newsquare: float32 [3072], P(('wshard', 'seq'))
- gate_update: float32 [3072], P(('wshard', 'seq'))
- outproj_grad: float32 [3072, 1536], P(('wshard', 'seq'))
- outproj_newmean: float32 [3072, 1536], P(('wshard', 'seq'))
- outproj_newsquare: float32 [3072, 1536], P(('wshard', 'seq'))
- outproj_update: float32 [3072, 1536], P(('wshard', 'seq'))
Inputs may be any that keep to these rules, and one draw needn't show every extreme that they name: `head_params`: row 0 holds logarithms of decay rates, row 1 step biases, row 2 skip factors.
All inputs are finite; a program needn't handle non-finite values.
Results may differ from a plain program's by a relative error of at most 0.012.
The roundings to bfloat16 on the way count: a program that leaves them out, or rounds other values in their place, can miss the bound.
Values may be sent and summed in bfloat16 or wider, within the bound.
No kernel may reach another device: no remote copies, remote signals or barrier semaphores. Data moves between devices by JAX's collectives and lax.ppermute only.
A program may use at most 256 MiB of HBM per device.

v0:
```python
import jax
import jax.numpy as jnp
from jax import lax
from jax.sharding import PartitionSpec as P

SPAN = 256


norm_eps = 1e-05
adam_eps = 1e-08
learn_rate = 0.02
beta_one = 0.9
beta_two = 0.999
first_fix = 1.0 - 0.9**10
second_fix = 1.0 - 0.999**10
highest = lax.Precision.HIGHEST


def depthwise(values, taps_all):
    kernel_len = taps_all.shape[0] - 1
    length = values.shape[0]
    padded = jnp.pad(values, ((kernel_len - 1, 0), (0, 0)))
    summed = taps_all[kernel_len] + taps_all[0] * padded[0:length]
    for offset in range(1, kernel_len):
        summed = summed + taps_all[offset] * padded[offset : offset + length]
    return summed


def state_scan(inputs, steps, rates, bmatrix, cmatrix):
    length, head_count, head_dim = inputs.shape
    blocks = length // SPAN
    xblock = inputs.reshape(blocks, SPAN, head_count, head_dim)
    dblock = steps.reshape(blocks, SPAN, head_count)
    bblock = bmatrix.reshape(blocks, SPAN, -1)
    cblock = cmatrix.reshape(blocks, SPAN, -1)
    within = jnp.cumsum(dblock * rates, axis=1)
    distance = within[:, :, None, :] - within[:, None, :, :]
    causal = (jnp.arange(SPAN)[:, None] >= jnp.arange(SPAN)[None, :])[None, :, :, None]
    mixing = jnp.exp(jnp.where(causal, distance, -jnp.inf))
    scores = jnp.einsum("cin,cjn->cij", cblock, bblock, precision=highest)
    weights = mixing * scores[:, :, :, None] * dblock[:, None, :, :]
    inside = jnp.einsum("cijh,cjhp->cihp", weights, xblock, precision=highest)
    final_log = within[:, -1, :]
    tail_scale = jnp.exp(final_log[:, None, :] - within) * dblock
    states = jnp.einsum(
        "cjn,cjhp->chpn", bblock, xblock * tail_scale[:, :, :, None], precision=highest
    )
    totals = jnp.cumsum(final_log, axis=0)
    between = (totals - final_log)[:, None, :] - totals[None, :, :]
    earlier = (jnp.arange(blocks)[:, None] > jnp.arange(blocks)[None, :])[:, :, None]
    carried = jnp.exp(jnp.where(earlier, between, -jnp.inf))
    incoming = jnp.einsum("kmh,mhpn->khpn", carried, states, precision=highest)
    outside = (
        jnp.einsum("cin,chpn->cihp", cblock, incoming, precision=highest)
        * jnp.exp(within)[:, :, :, None]
    )
    return (inside + outside).reshape(length, head_count, head_dim)


def mixer(values_in, shared_in, steps_in, taps_x, taps_shared, head_table):
    state_half = shared_in.shape[1] // 2
    length = values_in.shape[0]
    head_count = head_table.shape[1]
    x_active = jax.nn.silu(depthwise(values_in, taps_x))
    shared_active = jax.nn.silu(depthwise(shared_in, taps_shared))
    inputs = x_active.reshape(length, head_count, -1)
    steps = jax.nn.softplus(steps_in + head_table[1])
    rates = -jnp.exp(head_table[0])
    result = state_scan(
        inputs, steps, rates, shared_active[:, :state_half], shared_active[:, state_half:]
    )
    result = result + head_table[2][:, None] * inputs
    return result.reshape(length, -1)


def run_mixer(values_in, shared_in, steps_in, taps_x, taps_shared, head_table):
    return jax.vmap(mixer, in_axes=(0, 0, 0, None, None, None))(
        values_in, shared_in, steps_in, taps_x, taps_shared, head_table
    )


def adamw(grad, weight, first, second, decay):
    first_new = beta_one * first + (1.0 - beta_one) * grad
    second_new = beta_two * second + (1.0 - beta_two) * grad * grad
    update = -learn_rate * (
        first_new / first_fix / (jnp.sqrt(second_new / second_fix) + adam_eps) + decay * weight
    )
    return (grad, first_new, second_new, update)


def local(
    block_input,
    cotangent,
    norm_gain,
    norm_mean,
    norm_square,
    inproj_weight,
    inproj_mean,
    inproj_square,
    conv_params,
    conv_mean,
    conv_square,
    head_params,
    head_mean,
    head_square,
    gate_gain,
    gate_mean,
    gate_square,
    outproj_weight,
    outproj_mean,
    outproj_square,
):
    seq_devices = lax.axis_size("seq")
    seq_index = lax.axis_index("seq")
    shard_index = lax.axis_index("wshard")
    gain_all, inproj_all, conv_all, head_all, gate_all, outproj_all = (
        lax.all_gather(norm_gain, "wshard", axis=0, tiled=True),
        lax.all_gather(inproj_weight, "wshard", axis=0, tiled=True),
        lax.all_gather(conv_params, "wshard", axis=1, tiled=True),
        lax.all_gather(head_params, "wshard", axis=1, tiled=True),
        lax.all_gather(gate_gain, "wshard", axis=0, tiled=True),
        lax.all_gather(outproj_weight, "wshard", axis=0, tiled=True),
    )
    sequences, local_len, model_width = block_input.shape
    inner_width = gate_all.shape[0]
    head_count = head_all.shape[1]
    state_two = conv_all.shape[1] - inner_width
    full_len = local_len * seq_devices
    own_width = inner_width // seq_devices
    own_heads = head_count // seq_devices
    token_rows = sequences * local_len
    tokens = block_input.reshape(token_rows, model_width).astype(jnp.float32)
    scale = lax.rsqrt(jnp.mean(tokens * tokens, axis=-1, keepdims=True) + norm_eps)
    gain_f = gain_all.astype(jnp.float32)
    normed = (tokens * scale * gain_f).astype(jnp.bfloat16)
    projected = jnp.dot(normed, inproj_all, preferred_element_type=jnp.float32)
    gates = projected[:, :inner_width]
    x_send = (
        projected[:, inner_width : 2 * inner_width]
        .astype(jnp.bfloat16)
        .reshape(sequences, local_len, seq_devices, own_width)
    )
    shared_send = projected[:, 2 * inner_width : 2 * inner_width + state_two].astype(jnp.bfloat16)
    step_send = (
        projected[:, 2 * inner_width + state_two :]
        .astype(jnp.bfloat16)
        .reshape(sequences, local_len, seq_devices, own_heads)
    )
    x_recv, step_recv = (
        lax.all_to_all(x_send, "seq", split_axis=2, concat_axis=1, tiled=True),
        lax.all_to_all(step_send, "seq", split_axis=2, concat_axis=1, tiled=True),
    )
    shared_recv = lax.all_gather(
        shared_send.reshape(sequences, local_len, state_two), "seq", axis=1, tiled=True
    )
    conv_f = conv_all.astype(jnp.float32)
    taps_x = lax.dynamic_slice_in_dim(conv_f, seq_index * own_width, own_width, 1)
    taps_shared = conv_f[:, inner_width:]
    head_own = lax.dynamic_slice_in_dim(
        head_all.astype(jnp.float32), seq_index * own_heads, own_heads, 1
    )
    mixed, pull = jax.vjp(
        run_mixer,
        x_recv.reshape(sequences, full_len, own_width).astype(jnp.float32),
        shared_recv.astype(jnp.float32),
        step_recv.reshape(sequences, full_len, own_heads).astype(jnp.float32),
        taps_x,
        taps_shared,
        head_own,
    )
    back = lax.all_to_all(
        mixed.astype(jnp.bfloat16).reshape(sequences, full_len, 1, own_width),
        "seq",
        split_axis=1,
        concat_axis=2,
        tiled=True,
    )
    sent = back.reshape(token_rows, inner_width).astype(jnp.float32)
    sigma = jax.nn.sigmoid(gates)
    swish = gates * sigma
    gated = sent * swish
    grms = lax.rsqrt(jnp.mean(gated * gated, axis=-1, keepdims=True) + norm_eps)
    gate_f = gate_all.astype(jnp.float32)
    branch = (gated * grms * gate_f).astype(jnp.bfloat16)
    block_output = tokens + jnp.dot(branch, outproj_all, preferred_element_type=jnp.float32)
    seed = cotangent.reshape(token_rows, model_width)
    outproj_part = jnp.einsum("ti,td->id", branch, seed, preferred_element_type=jnp.float32)
    dbranch = jnp.einsum("td,id->ti", seed, outproj_all, preferred_element_type=jnp.float32)
    gate_part = jnp.sum(dbranch * gated * grms, axis=0)
    dscaled = dbranch * gate_f
    dgated = grms * dscaled - gated * grms * grms * grms * jnp.mean(
        dscaled * gated, axis=-1, keepdims=True
    )
    dsent = (dgated * swish).astype(jnp.bfloat16)
    dgates = dgated * sent * sigma * (1.0 + gates * (1.0 - sigma))
    dmixed = lax.all_to_all(
        dsent.reshape(sequences, local_len, seq_devices, own_width),
        "seq",
        split_axis=2,
        concat_axis=1,
        tiled=True,
    )
    d_values, d_shared, d_steps, d_taps_x, d_taps_shared, d_heads = pull(
        dmixed.reshape(sequences, full_len, own_width).astype(jnp.float32)
    )
    back_values, back_steps = (
        lax.all_to_all(
            d_values.astype(jnp.bfloat16).reshape(sequences, full_len, 1, own_width),
            "seq",
            split_axis=1,
            concat_axis=2,
            tiled=True,
        ),
        lax.all_to_all(
            d_steps.astype(jnp.bfloat16).reshape(sequences, full_len, 1, own_heads),
            "seq",
            split_axis=1,
            concat_axis=2,
            tiled=True,
        ),
    )
    shared_total = lax.psum_scatter(
        d_shared.astype(jnp.bfloat16), "seq", scatter_dimension=1, tiled=True
    ).astype(jnp.float32)
    dproj = jnp.concatenate(
        [
            dgates.astype(jnp.bfloat16),
            back_values.reshape(token_rows, inner_width),
            shared_total.reshape(token_rows, state_two).astype(jnp.bfloat16),
            back_steps.reshape(token_rows, head_count),
        ],
        axis=-1,
    )
    inproj_part = jnp.einsum("td,te->de", normed, dproj, preferred_element_type=jnp.float32)
    dnormed = jnp.einsum("te,de->td", dproj, inproj_all, preferred_element_type=jnp.float32)
    gain_part = jnp.sum(dnormed * tokens * scale, axis=0)
    dn_scaled = dnormed * gain_f
    input_grad = (
        seed.astype(jnp.float32)
        + scale * dn_scaled
        - tokens * scale * scale * scale * jnp.mean(dn_scaled * tokens, axis=-1, keepdims=True)
    )
    kernel_rows = conv_all.shape[0]
    x_zone = lax.dynamic_update_slice_in_dim(
        jnp.zeros((kernel_rows, inner_width), jnp.float32), d_taps_x, seq_index * own_width, 1
    )
    conv_part = jnp.concatenate([x_zone, d_taps_shared], axis=1)
    head_part = lax.dynamic_update_slice_in_dim(
        jnp.zeros((3, head_count), jnp.float32), d_heads, seq_index * own_heads, 1
    )
    grads = (gain_part, inproj_part, conv_part, gate_part, outproj_part)
    owned = (
        lax.psum_scatter(grads[0], ("wshard", "seq"), scatter_dimension=0, tiled=True),
        lax.psum_scatter(grads[1], ("wshard", "seq"), scatter_dimension=0, tiled=True),
        lax.psum_scatter(grads[2], ("wshard", "seq"), scatter_dimension=1, tiled=True),
        lax.psum_scatter(grads[3], ("wshard", "seq"), scatter_dimension=0, tiled=True),
        lax.psum_scatter(grads[4], ("wshard", "seq"), scatter_dimension=0, tiled=True),
    )
    head_total = lax.psum(head_part, ("wshard", "seq"))
    head_width = head_params.shape[1]
    head_grad = lax.dynamic_slice_in_dim(head_total, shard_index * head_width, head_width, 1)

    def own_piece(weight, count, axis_dim):
        return lax.dynamic_slice_in_dim(weight, seq_index * count, count, axis_dim).astype(
            jnp.float32
        )

    norm_res = adamw(
        owned[0], own_piece(norm_gain, norm_mean.shape[0], 0), norm_mean, norm_square, 0.0
    )
    inproj_res = adamw(
        owned[1], own_piece(inproj_weight, inproj_mean.shape[0], 0), inproj_mean, inproj_square, 0.1
    )
    conv_res = adamw(
        owned[2], own_piece(conv_params, conv_mean.shape[1], 1), conv_mean, conv_square, 0.0
    )
    head_res = adamw(head_grad, head_params.astype(jnp.float32), head_mean, head_square, 0.0)
    gate_res = adamw(
        owned[3], own_piece(gate_gain, gate_mean.shape[0], 0), gate_mean, gate_square, 0.0
    )
    outproj_res = adamw(
        owned[4],
        own_piece(outproj_weight, outproj_mean.shape[0], 0),
        outproj_mean,
        outproj_square,
        0.1,
    )
    return (
        block_output.reshape(sequences, local_len, model_width),
        input_grad.reshape(sequences, local_len, model_width),
        norm_res[0],
        norm_res[1],
        norm_res[2],
        norm_res[3],
        inproj_res[0],
        inproj_res[1],
        inproj_res[2],
        inproj_res[3],
        conv_res[0],
        conv_res[1],
        conv_res[2],
        conv_res[3],
        head_res[0],
        head_res[1],
        head_res[2],
        head_res[3],
        gate_res[0],
        gate_res[1],
        gate_res[2],
        gate_res[3],
        outproj_res[0],
        outproj_res[1],
        outproj_res[2],
        outproj_res[3],
    )


def solution(mesh):
    placed = (
        P("wshard", "seq", None),
        P("wshard", "seq", None),
        P("wshard"),
        P(("wshard", "seq")),
        P(("wshard", "seq")),
        P("wshard", None),
        P(("wshard", "seq"), None),
        P(("wshard", "seq"), None),
        P(None, "wshard"),
        P(None, ("wshard", "seq")),
        P(None, ("wshard", "seq")),
        P(None, "wshard"),
        P(None, "wshard"),
        P(None, "wshard"),
        P("wshard"),
        P(("wshard", "seq")),
        P(("wshard", "seq")),
        P("wshard", None),
        P(("wshard", "seq"), None),
        P(("wshard", "seq"), None),
    )
    return jax.shard_map(
        local,
        mesh=mesh,
        in_specs=placed,
        out_specs=(
            P("wshard", "seq", None),
            P("wshard", "seq", None),
            P(("wshard", "seq")),
            P(("wshard", "seq")),
            P(("wshard", "seq")),
            P(("wshard", "seq")),
            P(("wshard", "seq"), None),
            P(("wshard", "seq"), None),
            P(("wshard", "seq"), None),
            P(("wshard", "seq"), None),
            P(None, ("wshard", "seq")),
            P(None, ("wshard", "seq")),
            P(None, ("wshard", "seq")),
            P(None, ("wshard", "seq")),
            P(None, "wshard"),
            P(None, "wshard"),
            P(None, "wshard"),
            P(None, "wshard"),
            P(("wshard", "seq")),
            P(("wshard", "seq")),
            P(("wshard", "seq")),
            P(("wshard", "seq")),
            P(("wshard", "seq"), None),
            P(("wshard", "seq"), None),
            P(("wshard", "seq"), None),
            P(("wshard", "seq"), None),
        ),
        check_vma=False,
    )
```

profile of v0, /device:TPU:0, one launch (start us, length us, event | category | flops | bytes accessed | tf_op | source)
XLA Modules:
  0.0 1445.4 jit_solution(8524754652028090321)
XLA Ops:
  8.0 9.5 all-gather.1
  18.1 178.0 %all-gather.8.cloned.1.call-done = bf16[1536,6448]{0,1:T(8,128)(2,1)} async-done(((bf16[384,6448]{0,1:T(8,128)(2,1)}), bf16[1536,6448]{0,1:T(8,128)(2,1)}) %all-gather.8.cloned.1.call-update) | async-done | bytes 19808272 | tf_op jit(solution)/shard_map/all_gather | solution.py:118
  196.2 12.6 fusion.171
  212.1 8.0 all-gather.2
  220.2 7.3 all-gather
  229.2 4.6 all-to-all-start.1
  239.5 4.6 all-to-all-start
  244.9 14.5 %reduce-window.14 = f32[2,4,6,2,128]{4,3,2,1,0:T(2,128)S(1)} reduce-window(f32[2,4,6,2,128]{4,3,2,1,0:T(2,128)S(1)} %reshape.531, f32[]{:T(128)} %constant.40.clone.1), window={size=1x1x1x1x128 pad=0_0x0_0x0_0x0_0x127_0}, to_apply=%region_1.2 | reduce-window | flops 1560576 | bytes 98308 | tf_op jit(solution)/shard_map/reduce-window
  262.9 10.1 fusion.156
  274.8 3.2 fusion.172
  277.9 4.0 all-to-all-done
  284.2 3.1 fusion.33
  290.3 5.6 reshape.479
  295.9 5.5 fusion.36
  301.4 3.7 convolution_bitcast_fusion.1
  308.2 14.5 %bitcast_add_fusion.1 = f32[2,4,256,6,64]{2,4,3,1,0:T(8,128)S(1)} fusion(f32[2,4,256,6,64]{2,4,3,1,0:T(8,128)S(1)} %fusion.75, f32[2,4,256,6]{2,3,1,0:T(8,128)S(1)} %get-tuple-element.114, f32[2,4,256,256]{3,2,1,0:T(8,128)S(1)} %copy-done.22, f32[2,4,256,6]{2,3,1,0:T(8,128)S(1)} %bitcast.312, pred[256,256]{1,0:T(8,128)(4,1)S(1)} %iota_compare_fusion, ...), kind=kOutput, calls=%fused_computation.48 | convolution fusion | flops 2430074880 | bytes 11747328 | tf_op jit(solution)/shard_map/jvp(vmap(cijh,cjhp->cihp))/dot_general | solution.py:42
  322.7 3.7 copy.443
  326.4 5.4 reshape.486
  331.8 3.5 copy.444
  340.3 3.6 all-to-all-start.2
  344.0 8.1 all-gather.3
  352.1 29.6 %all-to-all-done.2 = bf16[2,1024,1,384]{3,0,2,1:T(2,128)(2,1)S(1)} async-done(((bf16[2,1024,1,384]{3,0,2,1:T(2,128)(2,1)}), bf16[2,1024,1,384]{3,0,2,1:T(2,128)(2,1)S(1)}, u32[]{:S(2)}, u32[]{:S(2)}) %all-to-all-start.2) | async-done | bytes 1572896 | tf_op jit(solution)/shard_map/all_to_all | solution.py:171
  382.2 3.4 copy.447
  385.6 3.9 multiply_reduce_fusion.8
  389.6 7.3 multiply_reduce_fusion.1
  396.9 5.1 fusion.30
  402.0 3.5 reshape.490
  405.5 4.8 copy.449
  410.3 4.3 all-to-all-start.3
  414.7 37.8 %all-to-all-done.3 = bf16[2,128,8,384]{3,1,0,2:T(8,128)(2,1)} async-done(((bf16[2,128,8,384]{3,1,0,2:T(8,128)(2,1)}), bf16[2,128,8,384]{3,1,0,2:T(8,128)(2,1)}, u32[]{:S(2)}, u32[]{:S(2)}) %all-to-all-start.3) | async-done | bytes 1572896 | tf_op jit(solution)/shard_map/all_to_all | solution.py:196
  458.1 4.1 reshape.491
  462.3 7.4 fusion.87
  474.0 3.9 convolution_bitcast_fusion
  478.0 5.5 fusion.82
  483.5 4.8 multiply_reduce_fusion.6
  488.3 13.9 fusion.8
  502.2 4.5 convolution_add_fusion.1
  514.3 18.5 %multiply_reduce_fusion.12 = (f32[256]{0:T(256)S(1)}, f32[256]{0:T(256)S(1)}, f32[256]{0:T(256)S(1)}, f32[256]{0:T(256)}, f32[256]{0:T(256)}, /*index=5*/f32[2,1024,256]{1,0,2:T(2,128)S(1)}) fusion(bf16[2,1024,256]{1,0,2:T(2,128)(2,1)} %all-gather.10.cloned.1.call-done, f32[2,1024,256]{1,0,2:T(2,128)} %copy-done.10, f32[2,1024,256]{1,0,2:T(2,128)} %get-tuple-element.91, ...), kind=kLoop, calls=%fused_computation.88 | loop fusion | flops 10484480 | bytes 9442304 | tf_op jit(solution)/shard_map/transpose(jvp(vmap()))/reduce_sum | solution.py:25
  535.3 7.4 fusion.45
  542.7 49.3 %copy.515 = bf16[2,1024,256]{0,2,1:T(8,128)(2,1)} copy(bf16[2,1024,256]{1,0,2:T(2,128)(2,1)} %fusion.45) | data formatting | bytes 2097152
  592.0 97.3 %reshape.535 = bf16[1024,512]{1,0:T(8,128)(2,1)} reshape(bf16[1024,256,2]{2,1,0:T(8,128)(2,1)} %bitcast.92) | data formatting | bytes 2097152
  689.4 10.3 bitcast_add_fusion
  699.7 3.7 copy.457
  703.4 5.2 reshape.492
  708.7 3.5 copy.458
  712.2 12.4 multiply_reduce_fusion.5
  725.5 9.4 fusion.155
  735.7 11.7 fusion.157
  752.9 60.4 %reduce-window.16 = f32[2,4,6,2,128]{4,3,2,1,0:T(2,128)S(1)} reduce-window(f32[2,4,6,2,128]{4,3,2,1,0:T(2,128)S(1)} %reshape.533, f32[]{:T(128)} %constant.40.clone.1), window={size=1x1x1x1x128 pad=0_0x0_0x0_0x0_0x0_127}, to_apply=%region_17.18 | reduce-window | flops 1560576 | bytes 98308 | tf_op jit(solution)/shard_map/reduce-window.2
  820.4 3.3 all-to-all-start.5
  830.4 5.0 all-to-all-start.4
  838.9 19.8 %reshape.536 = bf16[128,256,2]{2,1,0:T(8,128)(2,1)} reshape(bf16[128,512]{1,0:T(8,128)(2,1)} %reduce-scatter.11.cloned.1.call-done) | data formatting | bytes 262144
  858.7 8.7 copy.516
  867.4 6.2 all-to-all-done.4
  876.4 5.0 copy.461
  884.3 23.9 %fusion.112 = f32[1536,6448]{1,0:T(8,128)} fusion(bf16[256,1536]{1,0:T(8,128)(2,1)} %copy-done.18, bf16[256,48]{0,1:T(8,128)(2,1)S(1)} %bitcast.332, bf16[256,256]{0,1:T(8,128)(2,1)S(1)} %bitcast.323, bf16[256,3072]{0,1:T(8,128)(2,1)} %bitcast.301, bf16[256,3072]{0,1:T(8,128)(2,1)} %get-tuple-element.92), kind=kOutput, calls=%fused_computation.160 | convolution fusion | flops 5084119040 | bytes 43704320 | tf_op jit(solution)/shard_map/td,te->de/dot_general | solution.py:234
  908.2 3.7 constant_dynamic-slice_fusion.1
  914.4 8.5 convolution_add_fusion
  925.8 14.8 %fusion.58 = (f32[1536]{0:T(1024)S(1)}, f32[256]{0:T(256)S(1)}, f32[256,1536]{1,0:T(8,128)}) fusion(bf16[2,128,1536]{2,1,0:T(8,128)(2,1)} %param.20, f32[256]{0:T(256)S(1)} %copy-done.47, f32[1536]{0:T(1024)S(1)} %copy-done.33, bf16[1536,6448]{0,1:T(8,128)(2,1)} %all-gather.8.cloned.1.call-done, bf16[256,48]{0,1:T(8,128)(2,1)S(1)} %bitcast.333, ...), kind=kOutput, calls=%fused_computation.105 | convolution fusion | flops 5086869504 | bytes 25483264 | tf_op jit(solution)/shard_map/te,de->td/dot_general | solution.py:235
  940.7 39.7 %all-reduce.29 = (f32[1536]{0:T(1024)S(1)}, f32[3,48]{1,0:T(4,128)S(1)}, f32[3072]{0:T(1024)S(1)}) all-reduce(f32[1536]{0:T(1024)S(1)} %get-tuple-element.40, f32[3,48]{1,0:T(4,128)S(1)} %dynamic_update_slice.7, f32[3072]{0:T(1024)S(1)} %copy-done.45), channel_id=3, replica_groups=mesh['wshard'=4,'seq'=8] {'wshard','seq'}, use_global_device_ids=true, to_apply=%region_21.22.clone | all-reduce | flops 4752 | bytes 38016
  983.0 3.3 fusion.64
  986.3 76.4 %reduce-scatter.9.cloned.1.call-done = f32[96,1536]{1,0:T(8,128)} async-done(((f32[3072,1536]{1,0:T(8,128)}), f32[96,1536]{1,0:T(8,128)}) %reduce-scatter.9.cloned.1.call-update) | async-done | bytes 589840 | tf_op jit(solution)/shard_map/reduce_scatter | solution.py:257
  1065.6 368.4 %reduce-scatter.7.cloned.1.call-done = f32[48,6448]{1,0:T(8,128)} async-done(((f32[1536,6448]{1,0:T(8,128)}), f32[48,6448]{1,0:T(8,128)}) %reduce-scatter.7.cloned.1.call-update) | async-done | bytes 1238032 | tf_op jit(solution)/shard_map/reduce_scatter | solution.py:254
  1434.0 4.1 add_multiply_fusion
  (278 shorter events, 92.5 us)
Async XLA Ops:
  7.2 10.4 copy-start.14
  7.2 188.9 %all-gather.8.cloned.1.call-start = ((), (), s32[]{:S(2)}) async-start(), calls=%async_computation.9 | async-start | bytes 24760320 | tf_op jit(solution)/shard_map/all_gather | solution.py:118
  8.0 253.0 %all-gather.10.cloned.1.call-start = ((), (), s32[]{:S(2)}) async-start(), calls=%async_computation.10 | async-start | bytes 1179648 | tf_op jit(solution)/shard_map/all_gather | solution.py:153
  17.6 191.2 %copy-start.32 = (f32[1536]{0:T(1024)}, f32[1536]{0:T(1024)S(1)}, u32[]{:S(2)}) copy-start(f32[1536]{0:T(1024)S(1)} %reshape.520) | copy-start | bytes 18436
  17.9 190.9 %copy-start.46 = (f32[256]{0:T(256)}, f32[256]{0:T(256)S(1)}, u32[]{:S(2)}) copy-start(f32[256]{0:T(256)S(1)} %rsqrt_bitcast_fusion) | copy-start | bytes 3076
  18.1 190.7 %copy-start.18 = (bf16[256,1536]{1,0:T(8,128)(2,1)}, bf16[256,1536]{1,0:T(8,128)(2,1)S(1)}, u32[]{:S(2)}) copy-start(bf16[256,1536]{1,0:T(8,128)(2,1)S(1)} %fusion.61) | copy-start | bytes 2359300
  18.1 193.9 %copy-start.55 = (bf16[3,12]{1,0:T(4,128)(2,1)S(1)}, bf16[3,12]{1,0:T(4,128)(2,1)}, u32[]{:S(2)}) copy-start(bf16[3,12]{1,0:T(4,128)(2,1)} %param.31) | copy-start | bytes 220
  18.1 202.0 %copy-start.36 = (bf16[5,832]{1,0:T(8,128)(2,1)S(1)}, bf16[5,832]{1,0:T(8,128)(2,1)}, u32[]{:S(2)}) copy-start(bf16[5,832]{1,0:T(8,128)(2,1)} %param.28) | copy-start | bytes 24964
  211.3 178.3 %all-gather.12.cloned.1.call-start = ((), (), s32[]{:S(2)}) async-start(), calls=%async_computation.11 | async-start | bytes 11796480 | tf_op jit(solution)/shard_map/all_gather | solution.py:122
  227.7 56.5 %copy-start.40 = (f32[384]{0:T(512)}, f32[384]{0:T(512)S(1)}, u32[]{:S(2)}) copy-start(f32[384]{0:T(512)S(1)} %get-tuple-element.52) | copy-start | bytes 4612
  227.7 56.5 %copy-start.42 = (f32[384]{0:T(512)}, f32[384]{0:T(512)S(1)}, u32[]{:S(2)}) copy-start(f32[384]{0:T(512)S(1)} %get-tuple-element.53) | copy-start | bytes 4612
  227.7 56.5 %copy-start.43 = (f32[384]{0:T(512)}, f32[384]{0:T(512)S(1)}, u32[]{:S(2)}) copy-start(f32[384]{0:T(512)S(1)} %get-tuple-element.54) | copy-start | bytes 4612
  227.8 56.5 %copy-start.44 = (f32[384]{0:T(512)}, f32[384]{0:T(512)S(1)}, u32[]{:S(2)}) copy-start(f32[384]{0:T(512)S(1)} %get-tuple-element.55) | copy-start | bytes 4612
  227.8 17.0 %copy-start.50 = (f32[6]{0:T(128)}, f32[6]{0:T(128)S(1)}, u32[]{:S(2)}) copy-start(f32[6]{0:T(128)S(1)} %get-tuple-element.118) | copy-start | bytes 76
  227.8 33.0 %copy-start.37 = (f32[6]{0:T(128)}, f32[6]{0:T(128)S(1)}, u32[]{:S(2)}) copy-start(f32[6]{0:T(128)S(1)} %get-tuple-element.119) | copy-start | bytes 76
  229.2 10.3 all-to-all-start.1
  233.8 239.0 %copy-start.51 = (pred[4,4]{1,0:T(4,128)(4,1)}, pred[4,4]{1,0:T(4,128)(4,1)S(1)}, u32[]{:S(2)}) copy-start(pred[4,4]{1,0:T(4,128)(4,1)S(1)} %iota_compare_fusion.1) | copy-start | bytes 52
  239.5 42.5 %all-to-all-start = ((bf16[2,128,8,384]{3,1,0,2:T(8,128)(2,1)}), bf16[2,128,8,384]{3,1,0,2:T(8,128)(2,1)}, u32[]{:S(2)}, u32[]{:S(2)}) async-start(bf16[2,128,8,384]{3,1,0,2:T(8,128)(2,1)} %copy.422), calls=%async_computation | async-start | bytes 3145728 | tf_op jit(solution)/shard_map/all_to_all | solution.py:150
  244.8 16.1 %copy-start.25 = (f32[2,4,256,6]{2,1,3,0:T(4,128)}, f32[2,4,256,6]{2,1,3,0:T(4,128)S(1)}, u32[]{:S(2)}) copy-start(f32[2,4,256,6]{2,1,3,0:T(4,128)S(1)} %reshape.504) | copy-start | bytes 147460
  260.2 12.8 copy-start.30
  262.9 10.1 copy-start.10
  274.7 9.4 copy-start.7
  287.4 48.0 %copy-start = (f32[2,1024,384]{2,1,0:T(8,128)}, f32[2,1024,384]{2,1,0:T(8,128)S(1)}, u32[]{:S(2)}) copy-start(f32[2,1024,384]{2,1,0:T(8,128)S(1)} %get-tuple-element.88) | copy-start | bytes 9437188
  295.8 9.3 copy-start.8
  301.4 6.5 copy-start.13
  307.9 14.7 %copy-start.16 = (f32[2,4,256,6,64]{2,4,3,1,0:T(8,128)}, f32[2,4,256,6,64]{2,4,3,1,0:T(8,128)S(1)}, u32[]{:S(2)}) copy-start(f32[2,4,256,6,64]{2,4,3,1,0:T(8,128)S(1)} %fusion.75) | copy-start | bytes 9437188
  340.3 41.3 %all-to-all-start.2 = ((bf16[2,1024,1,384]{3,0,2,1:T(2,128)(2,1)}), bf16[2,1024,1,384]{3,0,2,1:T(2,128)(2,1)S(1)}, u32[]{:S(2)}, u32[]{:S(2)}) async-start(bf16[2,1024,1,384]{3,0,2,1:T(2,128)(2,1)} %copy.445), calls=%async_computation.2 | async-start | bytes 3145728 | tf_op jit(solution)/shard_map/all_to_all | solution.py:171
  389.6 7.3 copy-start.4
  410.3 42.1 %all-to-all-start.3 = ((bf16[2,128,8,384]{3,1,0,2:T(8,128)(2,1)}), bf16[2,128,8,384]{3,1,0,2:T(8,128)(2,1)}, u32[]{:S(2)}, u32[]{:S(2)}) async-start(bf16[2,128,8,384]{3,1,0,2:T(8,128)(2,1)} %copy.449), calls=%async_computation.3 | async-start | bytes 3145728 | tf_op jit(solution)/shard_map/all_to_all | solution.py:196
  414.6 424.3 %reduce-scatter.11.cloned.1.call-start = ((), (), s32[]{:S(2)}) async-start(), calls=%async_computation.14 | async-start | bytes 1179648
  462.3 7.4 copy-start.9
  462.3 7.4 copy-start.11
  469.7 8.3 copy-start.2
  689.4 234.9 %all-reduce.32.cloned.1.call-start = ((), (), s32[]{:S(2)}) async-start(), calls=%async_computation.15 | async-start | bytes 212992
  712.2 12.5 copy-start.53
  712.2 12.5 copy-start.54
  725.4 337.3 %reduce-scatter.9.cloned.1.call-start = ((), (), s32[]{:S(2)}) async-start(), calls=%async_computation.13 | async-start | bytes 19464192 | tf_op jit(solution)/shard_map/reduce_scatter | solution.py:257
  735.7 12.1 copy-start.26
  735.7 12.1 copy-start.31
  735.7 12.1 copy-start.38
  747.8 67.3 %copy-start.39 = (f32[6]{0:T(128)S(1)}, f32[6]{0:T(128)}, u32[]{:S(2)}) copy-start(f32[6]{0:T(128)} %copy-done.37) | copy-start | bytes 76
  749.8 74.0 %copy-start.41 = (f32[384]{0:T(512)S(1)}, f32[384]{0:T(512)}, u32[]{:S(2)}) copy-start(f32[384]{0:T(512)} %copy-done.40) | copy-start | bytes 4612
  820.4 10.1 all-to-all-start.5
  830.4 43.1 %all-to-all-start.4 = ((bf16[2,1024,1,384]{3,0,2,1:T(2,128)(2,1)}), bf16[2,1024,1,384]{3,0,2,1:T(2,128)(2,1)}, u32[]{:S(2)}, u32[]{:S(2)}) async-start(bf16[2,1024,1,384]{3,0,2,1:T(2,128)(2,1)} %copy.459), calls=%async_computation.4 | async-start | bytes 3145728 | tf_op jit(solution)/shard_map/all_to_all | solution.py:207
  835.4 598.5 %reduce-scatter.7.cloned.1.call-start = ((), (), s32[]{:S(2)}) async-start(), calls=%async_computation.12 | async-start | bytes 41361408 | tf_op jit(solution)/shard_map/reduce_scatter | solution.py:254
  914.4 8.6 copy-start.48
  914.4 9.9 copy-start.57
  914.4 9.9 copy-start.58
  914.4 11.3 copy-start.33
  914.4 11.3 copy-start.47
  925.7 15.0 %copy-start.45 = (f32[3072]{0:T(1024)S(1)}, f32[3072]{0:T(1024)}, u32[]{:S(2)}) copy-start(f32[3072]{0:T(1024)} %get-tuple-element.30) | copy-start | bytes 36868
  925.7 54.7 %copy-start.61 = (bf16[384]{0:T(512)(128)(2,1)S(1)}, bf16[384]{0:T(512)(128)(2,1)}, u32[]{:S(2)}) copy-start(bf16[384]{0:T(512)(128)(2,1)} %param.22) | copy-start | bytes 2308
  925.7 54.7 %copy-start.64 = (f32[48]{0:T(128)S(1)}, f32[48]{0:T(128)}, u32[]{:S(2)}) copy-start(f32[48]{0:T(128)} %param.24) | copy-start | bytes 580
  925.7 54.7 %copy-start.65 = (f32[48]{0:T(128)S(1)}, f32[48]{0:T(128)}, u32[]{:S(2)}) copy-start(f32[48]{0:T(128)} %param.23) | copy-start | bytes 580
  925.7 55.3 %copy-start.66 = (f32[96]{0:T(128)S(1)}, f32[96]{0:T(128)}, u32[]{:S(2)}) copy-start(f32[96]{0:T(128)} %param.36) | copy-start | bytes 1156
  925.8 55.3 %copy-start.67 = (f32[96]{0:T(128)S(1)}, f32[96]{0:T(128)}, u32[]{:S(2)}) copy-start(f32[96]{0:T(128)} %param.35) | copy-start | bytes 1156
  925.8 56.6 %copy-start.56 = (bf16[3,12]{1,0:T(4,128)(2,1)S(1)}, bf16[3,12]{1,0:T(4,128)(2,1)}, u32[]{:S(2)}) copy-start(bf16[3,12]{1,0:T(4,128)(2,1)} %param.31) | copy-start | bytes 220
  925.8 56.6 %copy-start.62 = (f32[3,12]{1,0:T(4,128)S(1)}, f32[3,12]{1,0:T(4,128)}, u32[]{:S(2)}) copy-start(f32[3,12]{1,0:T(4,128)} %param.33) | copy-start | bytes 436
  925.8 56.5 %copy-start.63 = (f32[3,12]{1,0:T(4,128)S(1)}, f32[3,12]{1,0:T(4,128)}, u32[]{:S(2)}) copy-start(f32[3,12]{1,0:T(4,128)} %param.32) | copy-start | bytes 436
  925.8 57.2 %copy-start.15 = (bf16[2,128,1536]{2,1,0:T(8,128)(2,1)S(1)}, bf16[2,128,1536]{2,1,0:T(8,128)(2,1)}, u32[]{:S(2)}) copy-start(bf16[2,128,1536]{2,1,0:T(8,128)(2,1)} %param.20) | copy-start | bytes 2359300
  925.8 57.2 %copy-start.20 = (bf16[2,128,1536]{2,1,0:T(8,128)(2,1)S(1)}, bf16[2,128,1536]{2,1,0:T(8,128)(2,1)}, u32[]{:S(2)}) copy-start(bf16[2,128,1536]{2,1,0:T(8,128)(2,1)} %param.21) | copy-start | bytes 2359300
  940.7 122.1 %copy-start.27 = (f32[96,1536]{1,0:T(8,128)S(1)}, f32[96,1536]{1,0:T(8,128)}, u32[]{:S(2)}) copy-start(f32[96,1536]{1,0:T(8,128)} %param.39) | copy-start | bytes 1769476
  983.0 451.0 %copy-start.21 = (bf16[48,6448]{1,0:T(8,128)(2,1)S(1)}, bf16[48,6448]{1,0:T(8,128)(2,1)}, u32[]{:S(2)}) copy-start(bf16[48,6448]{1,0:T(8,128)(2,1)} %copy.520) | copy-start | bytes 1857028
  986.3 447.7 %copy-start.24 = (f32[48,6448]{1,0:T(8,128)S(1)}, f32[48,6448]{1,0:T(8,128)}, u32[]{:S(2)}) copy-start(f32[48,6448]{1,0:T(8,128)} %param.27) | copy-start | bytes 3714052
  (17 other events, 52.1 us)
Sparse Core Ops, SparseCore 0:
  9.9 186.2 all-gather.7
  211.4 24.9 all-gather.9
  238.3 96.2 all-gather.11
  689.5 30.1 reduce-scatter.10
  725.7 119.9 all-reduce.31
  852.5 210.1 reduce-scatter.8
  1069.7 364.2 reduce-scatter.6
where the time goes:
time: 1450 us
  waiting for transfers between devices  703 us (48%)
  local copies, waits for them, and re-layouts  282 us (19%)
  matrix products  174 us (12%)
  other arithmetic  172 us (12%)
  blocking collectives  72.7 us (5%)
  starting transfers between devices  25.7 us (2%)
  between operations  15.8 us (1%)
    reduce_scatter x1, waiting for transfers between devices, local(): lax.psum_scatter(grads[1], ('wshard', 'seq'), scatter_dimension=0, tiled=...  368 us
    unnamed x149, local copies, waits for them, and re-layouts  190 us
    all_gather x1, waiting for transfers between devices, local(): lax.all_gather(inproj_weight, 'wshard', axis=0, tiled=True)  178 us
    another operation x8, other arithmetic  83.3 us
    reduce_scatter x1, waiting for transfers between devices, local(): lax.psum_scatter(grads[4], ('wshard', 'seq'), scatter_dimension=0, tiled=...  76.4 us
    unnamed x1, blocking collectives  39.7 us
    dot_general x3, matrix products, state_scan(): inside = jnp.einsum('cijh,cjhp->cihp', weights, xblock, precision=highest)  38.7 us
    all_to_all x1, waiting for transfers between devices, local(): lax.all_to_all(dsent.reshape(sequences, local_len, seq_devices, own_width...  37.8 us
  transfers between devices with their start and end apart: 13, of which 8 were waited for; matrix products, arithmetic and copies ran while one was open for 24% of the time, Pallas kernels for 0%

commit v1 on v0

v1 whole, which is shorter than its diff:
```python
import functools

import jax
import jax.numpy as jnp
from jax import lax
from jax.experimental import pallas as pl
from jax.experimental.pallas import tpu as pltpu
from jax.sharding import PartitionSpec as P

norm_eps = 1e-05
adam_eps = 1e-08
learn_rate = 0.02
beta_one = 0.9
beta_two = 0.999
first_fix = 1.0 - 0.9**10
second_fix = 1.0 - 0.999**10

f32 = jnp.float32
bf16 = jnp.bfloat16
Q = 128
HP = 16
FLOOR = -1e30
VMEM_LIMIT = 56 * 1024 * 1024


def dot_nn(a, b):
    return lax.dot_general(a, b, (((1,), (0,)), ((), ())), preferred_element_type=f32)


def dot_nt(a, b):
    return lax.dot_general(a, b, (((1,), (1,)), ((), ())), preferred_element_type=f32)


def dot_tn(a, b):
    return lax.dot_general(a, b, (((0,), (0,)), ((), ())), preferred_element_type=f32)


def sigmoid(a):
    return 1.0 / (1.0 + jnp.exp(-a))


def lanes(shape):
    return lax.broadcasted_iota(jnp.int32, shape, 1)


def earlier_by(current, previous, lane, shift):
    return pltpu.roll(jnp.where(lane >= Q - shift, previous, current), shift, 1)


def later_by(current, following, lane, shift):
    return pltpu.roll(jnp.where(lane < shift, following, current), Q - shift, 1)


def running_sum(a, lane):
    shift = 1
    while shift < Q:
        a = a + jnp.where(lane >= shift, pltpu.roll(a, shift, 1), 0.0)
        shift *= 2
    return a


def running_sum_back(a, lane):
    shift = 1
    while shift < Q:
        a = a + jnp.where(lane < Q - shift, pltpu.roll(a, Q - shift, 1), 0.0)
        shift *= 2
    return a


def mixer_forward(
    own_width,
    heads,
    kernel_len,
    order_ref,
    normed_ref,
    weight_ref,
    chan_ref,
    head_ref,
    gates_ref,
    values_ref,
    conv_ref,
    sent_ref,
    table_ref,
    state_ref,
    before,
    state,
    active,
    steps,
    inter,
    scaled,
):
    channels = chan_ref.shape[0]
    width = own_width // heads
    token_block = normed_ref.shape[0]

    @pl.when(pl.program_id(0) == 0)
    def _():
        before[...] = jnp.zeros_like(before)
        state[...] = jnp.zeros_like(state)

    normed = normed_ref[...]
    gates_ref[...] = dot_nt(weight_ref[0:own_width, :], normed)
    values_ref[...] = dot_nt(weight_ref[own_width : own_width + channels, :], normed).astype(bf16)
    steps[...] = dot_nt(weight_ref[own_width + channels :, :], normed).astype(bf16).astype(f32)
    lane = lanes((Q, Q))
    lane_head = lanes((HP, Q))
    causal = lax.broadcasted_iota(jnp.int32, (Q, Q), 0) <= lane

    def block(at, carry):
        here = pl.ds(pl.multiple_of(at * Q, Q), Q)

        def convolve(tile, inner):
            rows = pl.ds(pl.multiple_of(tile * Q, Q), Q)
            raw = values_ref[rows, here]
            current = raw.astype(f32)
            previous = before[rows, :].astype(f32)
            taps = chan_ref[rows, :]
            out = taps[:, kernel_len : kernel_len + 1] + taps[:, kernel_len - 1 : kernel_len] * current
            for shift in range(1, kernel_len):
                tap = kernel_len - 1 - shift
                out = out + taps[:, tap : tap + 1] * earlier_by(current, previous, lane, shift)
            before[rows, :] = raw
            conv_ref[rows, here] = out
            active[rows, :] = out * sigmoid(out)
            return inner

        lax.fori_loop(0, channels // Q, convolve, 0)
        drive = steps[:, here] + head_ref[:, 1:2]
        step = jnp.maximum(drive, 0.0) + jnp.log1p(jnp.exp(-jnp.abs(drive)))
        within = running_sum(step * head_ref[:, 0:1], lane_head)
        table_ref[0, :, here] = step
        table_ref[1, :, here] = within
        table_ref[2, :, here] = sigmoid(drive)
        within_col = jnp.transpose(within)
        total = within[:, Q - 1 : Q]
        grow = jnp.exp(within)
        tail = jnp.exp(total - within) * step
        total_decay = jnp.exp(total)
        b_rows = jnp.transpose(active[own_width : own_width + Q, :]).astype(bf16)
        c_cols = active[own_width + Q : own_width + 2 * Q, :].astype(bf16)
        scores = dot_nn(b_rows, c_cols)
        held = state[...].astype(bf16)
        state_ref[at] = held
        inter[...] = dot_nn(held, c_cols)
        for head in range(heads):
            rows = slice(head * width, (head + 1) * width)
            x = active[rows, :]
            decay = jnp.exp(
                jnp.where(causal, within[head : head + 1, :] - within_col[:, head : head + 1], FLOOR)
            )
            weights = (decay * scores).astype(bf16)
            driven = (x * step[head : head + 1, :]).astype(bf16)
            mixed = dot_nn(driven, weights)
            mixed = mixed + inter[rows, :] * grow[head : head + 1, :]
            mixed = mixed + chan_ref[rows, 6:7] * x
            sent_ref[rows, here] = mixed.astype(bf16)
            scaled[rows, :] = (x * tail[head : head + 1, :]).astype(bf16)
            state[rows, :] = state[rows, :] * total_decay[head : head + 1, :]
        state[...] += dot_nn(scaled[...], b_rows)
        return carry

    lax.fori_loop(0, token_block // Q, block, 0)


def gate_statistics(order_ref, gates_ref, sent_ref, cot_ref, weight_ref, chan_ref, dbranch_ref, stat_ref):
    dbranch = dot_nt(weight_ref[...], cot_ref[...])
    dbranch_ref[...] = dbranch
    gates = gates_ref[...]
    gated = sent_ref[...].astype(f32) * (gates * sigmoid(gates))
    square = jnp.sum(gated * gated, axis=0, keepdims=True)
    cross = jnp.sum(gated * (dbranch * chan_ref[0 : gates.shape[0], 7:8]), axis=0, keepdims=True)
    stat_ref[...] = jnp.concatenate([square, cross, jnp.zeros((6, square.shape[1]), f32)], axis=0)


def mixer_backward(
    own_width,
    heads,
    kernel_len,
    order_ref,
    gates_ref,
    sent_ref,
    dbranch_ref,
    conv_ref,
    values_ref,
    table_ref,
    state_ref,
    stat_ref,
    chan_ref,
    head_ref,
    dproj_ref,
    branch_ref,
    conv_acc,
    head_acc,
    adjoint,
    following,
    active,
    dactive,
    dsent,
    inter,
    reach,
    driven,
    tailed,
    rows_scr,
):
    channels = chan_ref.shape[0]
    width = own_width // heads
    token_block = gates_ref.shape[1]

    @pl.when(pl.program_id(0) == 0)
    def _():
        adjoint[...] = jnp.zeros_like(adjoint)
        following[...] = jnp.zeros_like(following)
        conv_acc[...] = jnp.zeros_like(conv_acc)
        head_acc[...] = jnp.zeros_like(head_acc)
        rows_scr[...] = jnp.zeros_like(rows_scr)

    lane = lanes((Q, Q))
    sub = lax.broadcasted_iota(jnp.int32, (Q, Q), 0)
    lane_head = lanes((HP, Q))
    causal = sub >= lane
    strict = (sub < lane).astype(bf16)

    def block(index, carry):
        at = token_block // Q - 1 - index
        here = pl.ds(pl.multiple_of(at * Q, Q), Q)
        grms = stat_ref[0:1, here]
        pull = stat_ref[1:2, here]

        def gate(tile, inner):
            rows = pl.ds(pl.multiple_of(tile * Q, Q), Q)
            gates = gates_ref[rows, here]
            sent = sent_ref[rows, here].astype(f32)
            gain = chan_ref[rows, 7:8]
            sig = sigmoid(gates)
            swish = gates * sig
            gated = sent * swish
            dgated = grms * (dbranch_ref[rows, here] * gain - gated * pull)
            dsent[rows, :] = (dgated * swish).astype(bf16)
            dproj_ref[rows, here] = (dgated * sent * sig * (1.0 + gates * (1.0 - sig))).astype(bf16)
            branch_ref[rows, here] = (gated * grms * gain).astype(bf16)
            return inner

        lax.fori_loop(0, own_width // Q, gate, 0)

        def activate(tile, inner):
            rows = pl.ds(pl.multiple_of(tile * Q, Q), Q)
            conv = conv_ref[rows, here]
            active[rows, :] = conv * sigmoid(conv)
            return inner

        lax.fori_loop(0, channels // Q, activate, 0)
        step = table_ref[0, :, here]
        within = table_ref[1, :, here]
        within_col = jnp.transpose(within)
        total = within[:, Q - 1 : Q]
        grow = jnp.exp(within)
        fade = jnp.exp(total - within)
        tail = fade * step
        total_decay = jnp.exp(total)
        b_cols_f = active[own_width : own_width + Q, :]
        c_cols_f = active[own_width + Q : own_width + 2 * Q, :]
        b_cols = b_cols_f.astype(bf16)
        c_cols = c_cols_f.astype(bf16)
        c_rows = jnp.transpose(c_cols_f).astype(bf16)
        scores = dot_nn(c_rows, b_cols)
        held = state_ref[at]
        after = adjoint[...].astype(bf16)
        inter[...] = dot_nn(held, c_cols)
        reach[...] = dot_nn(after, b_cols)
        dscores = jnp.zeros((Q, Q), f32)
        blank = jnp.zeros((width, Q), bf16)
        for pair in range(heads // 2):
            turned = jnp.transpose(dsent[pair * 2 * width : (pair + 1) * 2 * width, :].astype(f32)).astype(bf16)
            for half in range(2):
                head = 2 * pair + half
                rows = slice(head * width, (head + 1) * width)
                one = slice(head, head + 1)
                x = active[rows, :]
                x_low = x.astype(bf16)
                grad_low = dsent[rows, :]
                grad = grad_low.astype(f32)
                decay = jnp.exp(
                    jnp.where(causal, within_col[:, head : head + 1] - within[one, :], FLOOR)
                )
                lone = jnp.concatenate([x_low, blank] if half == 0 else [blank, x_low], axis=0)
                dweights = dot_nn(turned, lone)
                spread = decay * dweights * step[one, :]
                dscores = dscores + spread
                crossing = dot_nn((spread * scores).astype(bf16), strict)
                rows_scr[0, one, :] = jnp.sum(jnp.where(causal, crossing, 0.0), axis=0, keepdims=True)
                far = reach[rows, :]
                back = dot_nn(grad_low, (decay * scores).astype(bf16)) + far * fade[one, :]
                rows_scr[1, one, :] = jnp.sum(x * back, axis=0, keepdims=True)
                rows_scr[2, one, :] = jnp.sum(x * far, axis=0, keepdims=True) * tail[one, :]
                rows_scr[3, one, :] = jnp.sum(grad * inter[rows, :], axis=0, keepdims=True) * grow[one, :]
                rows_scr[4, one, :] = jnp.sum(grad * x, axis=0, keepdims=True)
                old = adjoint[rows, :]
                rows_scr[5, one, :] = jnp.sum(old * held[rows, :].astype(f32), axis=0, keepdims=True)
                dactive[rows, :] = back * step[one, :] + chan_ref[rows, 6:7] * grad
                driven[rows, :] = (grad * grow[one, :]).astype(bf16)
                tailed[rows, :] = (x * tail[one, :]).astype(bf16)
                adjoint[rows, :] = old * total_decay[one, :]
        dlow = dscores.astype(bf16)
        dactive[own_width : own_width + Q, :] = dot_nn(c_cols, dlow) + dot_tn(after, tailed[...])
        dactive[own_width + Q : own_width + 2 * Q, :] = dot_nt(b_cols, dlow) + dot_tn(held, driven[...])
        adjoint[...] += dot_nn(driven[...], c_rows)
        ahead = rows_scr[2]
        dlog = (
            rows_scr[0]
            + running_sum_back(rows_scr[3], lane_head)
            + (running_sum(ahead, lane_head) - ahead)
            + total_decay * jnp.sum(rows_scr[5], axis=1, keepdims=True)
        )
        dstep = (rows_scr[1] + head_ref[:, 0:1] * dlog) * table_ref[2, :, here]
        dproj_ref[own_width + channels :, here] = dstep.astype(bf16)
        head_acc[0] += step * dlog
        head_acc[1] += dstep
        head_acc[2] += rows_scr[4]

        def convolve(tile, inner):
            rows = pl.ds(pl.multiple_of(tile * Q, Q), Q)
            conv = conv_ref[rows, here]
            sig = sigmoid(conv)
            dconv = dactive[rows, :] * sig * (1.0 + conv * (1.0 - sig))
            taps = chan_ref[rows, :]
            raw = values_ref[rows, here].astype(f32)
            nxt = following[rows, :]
            dvalue = taps[:, kernel_len - 1 : kernel_len] * dconv
            conv_acc[kernel_len - 1, rows, :] += raw * dconv
            for shift in range(1, kernel_len):
                tap = kernel_len - 1 - shift
                moved = later_by(dconv, nxt, lane, shift)
                dvalue = dvalue + taps[:, tap : tap + 1] * moved
                conv_acc[tap, rows, :] += raw * moved
            conv_acc[kernel_len, rows, :] += dconv
            following[rows, :] = dconv
            dproj_ref[pl.ds(pl.multiple_of(own_width + tile * Q, Q), Q), here] = dvalue.astype(bf16)
            return inner

        lax.fori_loop(0, channels // Q, convolve, 0)
        return carry

    lax.fori_loop(0, token_block // Q, block, 0)


def run_forward(order, normed, weight, chan, head_table, own_width, heads, kernel_len):
    places, token_block, model_width = normed.shape
    channels = chan.shape[0]
    full = places * token_block
    fixed = lambda k, order: (0, 0)
    cols = lambda k, order: (0, k)
    spec = pltpu.PrefetchScalarGridSpec(
        num_scalar_prefetch=1,
        grid=(places,),
        in_specs=[
            pl.BlockSpec((None, token_block, model_width), lambda k, order: (order[k], 0, 0)),
            pl.BlockSpec(weight.shape, fixed),
            pl.BlockSpec(chan.shape, fixed),
            pl.BlockSpec(head_table.shape, fixed),
        ],
        out_specs=[
            pl.BlockSpec((own_width, token_block), cols),
            pl.BlockSpec((channels, token_block), cols),
            pl.BlockSpec((channels, token_block), cols),
            pl.BlockSpec((own_width, token_block), cols),
            pl.BlockSpec((3, HP, token_block), lambda k, order: (0, 0, k)),
            pl.BlockSpec((token_block // Q, own_width, Q), lambda k, order: (k, 0, 0)),
        ],
        scratch_shapes=[
            pltpu.VMEM((channels, Q), bf16),
            pltpu.VMEM((own_width, Q), f32),
            pltpu.VMEM((channels, Q), f32),
            pltpu.VMEM((HP, token_block), f32),
            pltpu.VMEM((own_width, Q), f32),
            pltpu.VMEM((own_width, Q), bf16),
        ],
    )
    flops = 2 * full * model_width * weight.shape[0]
    return pl.pallas_call(
        functools.partial(mixer_forward, own_width, heads, kernel_len),
        grid_spec=spec,
        out_shape=[
            jax.ShapeDtypeStruct((own_width, full), f32),
            jax.ShapeDtypeStruct((channels, full), bf16),
            jax.ShapeDtypeStruct((channels, full), f32),
            jax.ShapeDtypeStruct((own_width, full), bf16),
            jax.ShapeDtypeStruct((3, HP, full), f32),
            jax.ShapeDtypeStruct((full // Q, own_width, Q), bf16),
        ],
        compiler_params=pltpu.CompilerParams(
            dimension_semantics=("arbitrary",), vmem_limit_bytes=VMEM_LIMIT
        ),
        cost_estimate=pl.CostEstimate(
            flops=2 * flops, bytes_accessed=24 * 1024 * 1024, transcendentals=4 * 1024 * 1024
        ),
        name="mixer_forward",
    )(order, normed, weight, chan, head_table)


def run_statistics(order, gates, sent, cotangent, weight, chan):
    places, token_block, model_width = cotangent.shape
    own_width, full = gates.shape
    fixed = lambda k, order: (0, 0)
    cols = lambda k, order: (0, k)
    spec = pltpu.PrefetchScalarGridSpec(
        num_scalar_prefetch=1,
        grid=(places,),
        in_specs=[
            pl.BlockSpec((own_width, token_block), cols),
            pl.BlockSpec((own_width, token_block), cols),
            pl.BlockSpec((None, token_block, model_width), lambda k, order: (order[k], 0, 0)),
            pl.BlockSpec(weight.shape, fixed),
            pl.BlockSpec(chan.shape, fixed),
        ],
        out_specs=[
            pl.BlockSpec((own_width, token_block), cols),
            pl.BlockSpec((8, token_block), cols),
        ],
    )
    return pl.pallas_call(
        gate_statistics,
        grid_spec=spec,
        out_shape=[
            jax.ShapeDtypeStruct((own_width, full), f32),
            jax.ShapeDtypeStruct((8, full), f32),
        ],
        compiler_params=pltpu.CompilerParams(
            dimension_semantics=("arbitrary",), vmem_limit_bytes=VMEM_LIMIT
        ),
        cost_estimate=pl.CostEstimate(
            flops=2 * full * model_width * own_width,
            bytes_accessed=16 * 1024 * 1024,
            transcendentals=own_width * full,
        ),
        name="gate_statistics",
    )(order, gates, sent, cotangent, weight, chan)


def run_backward(
    order, gates, sent, dbranch, conv, values, table, states, stats, chan, head_table, heads, kernel_len, places
):
    own_width, full = gates.shape
    channels = chan.shape[0]
    token_block = full // places
    out_rows = own_width + channels + HP
    last = places - 1
    fixed = lambda k, order: (0, 0)
    cols = lambda k, order: (0, last - k)
    turned = lambda k, order: (0, order[last - k])
    spec = pltpu.PrefetchScalarGridSpec(
        num_scalar_prefetch=1,
        grid=(places,),
        in_specs=[
            pl.BlockSpec((own_width, token_block), cols),
            pl.BlockSpec((own_width, token_block), cols),
            pl.BlockSpec((own_width, token_block), cols),
            pl.BlockSpec((channels, token_block), cols),
            pl.BlockSpec((channels, token_block), cols),
            pl.BlockSpec((3, HP, token_block), lambda k, order: (0, 0, last - k)),
            pl.BlockSpec((token_block // Q, own_width, Q), lambda k, order: (last - k, 0, 0)),
            pl.BlockSpec((8, token_block), cols),
            pl.BlockSpec(chan.shape, fixed),
            pl.BlockSpec(head_table.shape, fixed),
        ],
        out_specs=[
            pl.BlockSpec((out_rows, token_block), turned),
            pl.BlockSpec((own_width, token_block), turned),
            pl.BlockSpec((kernel_len + 1, channels, Q), lambda k, order: (0, 0, 0)),
            pl.BlockSpec((3, HP, Q), lambda k, order: (0, 0, 0)),
        ],
        scratch_shapes=[
            pltpu.VMEM((own_width, Q), f32),
            pltpu.VMEM((channels, Q), f32),
            pltpu.VMEM((channels, Q), f32),
            pltpu.VMEM((channels, Q), f32),
            pltpu.VMEM((own_width, Q), bf16),
            pltpu.VMEM((own_width, Q), f32),
            pltpu.VMEM((own_width, Q), f32),
            pltpu.VMEM((own_width, Q), bf16),
            pltpu.VMEM((own_width, Q), bf16),
            pltpu.VMEM((6, HP, Q), f32),
        ],
    )
    return pl.pallas_call(
        functools.partial(mixer_backward, own_width, heads, kernel_len),
        grid_spec=spec,
        out_shape=[
            jax.ShapeDtypeStruct((out_rows, full), bf16),
            jax.ShapeDtypeStruct((own_width, full), bf16),
            jax.ShapeDtypeStruct((kernel_len + 1, channels, Q), f32),
            jax.ShapeDtypeStruct((3, HP, Q), f32),
        ],
        compiler_params=pltpu.CompilerParams(
            dimension_semantics=("arbitrary",), vmem_limit_bytes=VMEM_LIMIT
        ),
        cost_estimate=pl.CostEstimate(
            flops=16 * 1024 * 1024 * 1024, bytes_accessed=32 * 1024 * 1024, transcendentals=4 * 1024 * 1024
        ),
        name="mixer_backward",
    )(order, gates, sent, dbranch, conv, values, table, states, stats, chan, head_table)


def adamw(grad, weight, first, second, decay):
    first_new = beta_one * first + (1.0 - beta_one) * grad
    second_new = beta_two * second + (1.0 - beta_two) * grad * grad
    update = -learn_rate * (
        first_new / first_fix / (jnp.sqrt(second_new / second_fix) + adam_eps) + decay * weight
    )
    return (grad, first_new, second_new, update)


def pieces_for(stacked, index):
    return lax.dynamic_index_in_dim(stacked, index, 0, keepdims=False)


def local(
    block_input,
    cotangent,
    norm_gain,
    norm_mean,
    norm_square,
    inproj_weight,
    inproj_mean,
    inproj_square,
    conv_params,
    conv_mean,
    conv_square,
    head_params,
    head_mean,
    head_square,
    gate_gain,
    gate_mean,
    gate_square,
    outproj_weight,
    outproj_mean,
    outproj_square,
):
    group = lax.axis_size("seq")
    shards = lax.axis_size("wshard")
    seq_index = lax.axis_index("seq")
    shard = lax.axis_index("wshard")
    places = group // 2
    place = seq_index // 2
    core = seq_index % 2
    sequences, local_len, model_width = block_input.shape
    inner_width = gate_gain.shape[0] * shards
    head_count = head_params.shape[1] * shards
    kernel_len = conv_params.shape[0] - 1
    state_two = conv_params.shape[1] * shards - inner_width
    if sequences != 2 or places != shards or state_two != 2 * Q:
        raise ValueError("unexpected sizes")
    own_width = inner_width // places
    heads = head_count // places
    width = inner_width // head_count

    def swap(x):
        return lax.ppermute(x, "seq", [(i, i ^ 1) for i in range(group)])

    def along(x, step):
        return lax.ppermute(
            x, "seq", [(i, (i - 2 * step) % group) for i in range(group)]
        )

    def across(x, mask):
        return lax.ppermute(x, "wshard", [(i, i ^ mask) for i in range(shards)])

    def shard_gather(x):
        found = jnp.stack([x] + [across(x, mask) for mask in range(1, shards)])
        return jnp.stack([pieces_for(found, shard ^ k) for k in range(shards)])

    small = jnp.concatenate(
        [norm_gain, gate_gain, conv_params.reshape(-1), head_params.reshape(-1)]
    )
    small_all = shard_gather(small)
    at_gate = norm_gain.shape[0]
    at_conv = at_gate + gate_gain.shape[0]
    at_head = at_conv + conv_params.size
    gain_f = small_all[:, :at_gate].reshape(-1).astype(f32)
    gate_f = small_all[:, at_gate:at_conv].reshape(-1).astype(f32)
    conv_f = (
        small_all[:, at_conv:at_head]
        .reshape(shards, kernel_len + 1, -1)
        .transpose(1, 0, 2)
        .reshape(kernel_len + 1, -1)
        .astype(f32)
    )
    head_f = (
        small_all[:, at_head:].reshape(shards, 3, -1).transpose(1, 0, 2).reshape(3, -1).astype(f32)
    )
    taps = jnp.concatenate(
        [
            lax.dynamic_slice_in_dim(conv_f, place * own_width, own_width, 1),
            conv_f[:, inner_width:],
        ],
        axis=1,
    )
    channels = taps.shape[1]
    head_own = lax.dynamic_slice_in_dim(head_f, place * heads, heads, 1)
    gate_own = lax.dynamic_slice_in_dim(gate_f, place * own_width, own_width, 0)
    skip_gain = jnp.pad(
        jnp.stack([jnp.repeat(head_own[2], width), gate_own]), ((0, 0), (0, state_two))
    )
    chan = jnp.concatenate(
        [taps, jnp.zeros((6 - taps.shape[0], channels), f32), skip_gain], axis=0
    ).T
    rates = -jnp.exp(head_own[0])
    head_table = jnp.pad(
        jnp.stack([rates, head_own[1]], axis=1), ((0, HP - heads), (0, Q - 2))
    )

    tokens = block_input.astype(f32)
    scale = lax.rsqrt(jnp.mean(tokens * tokens, axis=-1, keepdims=True) + norm_eps)
    normed = (tokens * scale * gain_f).astype(bf16)

    def join(kept, other):
        return jnp.where(core == 0, jnp.concatenate([kept, other]), jnp.concatenate([other, kept]))

    def to_sequence(x):
        kept = lax.dynamic_index_in_dim(x, core, 0, keepdims=False)
        other = swap(lax.dynamic_index_in_dim(x, 1 - core, 0, keepdims=False))
        return join(kept, other)

    def to_tokens(x):
        halves = x.reshape(2, local_len, -1)
        kept = lax.dynamic_index_in_dim(halves, core, 0, keepdims=True)
        other = swap(lax.dynamic_index_in_dim(halves, 1 - core, 0, keepdims=True))
        return join(kept, other)

    def line_gather(x):
        return jnp.stack([x] + [along(x, step) for step in range(1, places)])

    def in_order(found):
        stacked = jnp.stack(found)
        return jnp.stack([pieces_for(stacked, (place - k) % places) for k in range(places)])

    order = (jnp.arange(places, dtype=jnp.int32) - place) % places
    normed_all = line_gather(to_sequence(normed))
    cot_all = line_gather(to_sequence(cotangent))

    half_cols = jnp.concatenate(
        [
            lax.dynamic_slice_in_dim(
                inproj_weight, core * inner_width + place * own_width, own_width, 1
            ),
            lax.dynamic_slice_in_dim(inproj_weight, 2 * inner_width + core * Q, Q, 1),
            jnp.pad(
                lax.dynamic_slice_in_dim(
                    inproj_weight, 2 * inner_width + state_two + place * heads, heads, 1
                ),
                ((0, 0), (0, HP - heads)),
            ),
        ],
        axis=1,
    ).T
    found = shard_gather(half_cols)
    half = found.transpose(1, 0, 2).reshape(half_cols.shape[0], model_width)
    other_half = swap(half)
    first = jnp.where(core == 0, half, other_half)
    second = jnp.where(core == 0, other_half, half)
    weight = jnp.concatenate(
        [
            first[:own_width],
            second[:own_width],
            first[own_width : own_width + Q],
            second[own_width : own_width + Q],
            half[own_width + Q :],
        ]
    )
    outproj_all = lax.all_gather(outproj_weight, "wshard", axis=0, tiled=True)
    outproj_own = lax.dynamic_slice_in_dim(outproj_all, place * own_width, own_width, 0)

    gates, values, conv, sent, table, states = run_forward(
        order, normed_all, weight, chan, head_table, own_width, heads, kernel_len
    )
    dbranch, stat = run_statistics(order, gates, sent, cot_all, outproj_own, chan)
    stat = stat[:2]
    stat = stat + sum(along(stat, step) for step in range(1, places))
    grms = lax.rsqrt(stat[0] / inner_width + norm_eps)
    stats = jnp.pad(
        jnp.stack([grms, grms * grms * (stat[1] / inner_width)]), ((0, 6), (0, 0))
    )
    dproj, branch, conv_acc, head_acc = run_backward(
        order, gates, sent, dbranch, conv, values, table, states, stats, chan, head_table,
        heads, kernel_len, places,
    )
    token_block = 2 * local_len
    flat = places * token_block

    def columns(x, m):
        return x[:, m * token_block : (m + 1) * token_block]

    branch_all = in_order([along(columns(branch, m), -m) if m else columns(branch, 0) for m in range(places)])
    out = dot_tn(branch_all.reshape(inner_width, token_block), outproj_all)
    block_output = tokens + to_tokens(out)

    dnormed_part = lax.dot_general(
        dproj, weight, (((0,), (0,)), ((), ())), preferred_element_type=f32
    ).astype(bf16)
    dnormed = dnormed_part[:token_block].astype(f32)
    for m in range(1, places):
        dnormed = dnormed + along(dnormed_part[m * token_block : (m + 1) * token_block], -m).astype(f32)
    dn_scaled = to_tokens(dnormed) * gain_f
    input_grad = (
        cotangent.astype(f32)
        + scale * dn_scaled
        - tokens * scale * scale * scale * jnp.mean(dn_scaled * tokens, axis=-1, keepdims=True)
    )

    def over_cores(x, axis):
        kept = lax.dynamic_index_in_dim(x, core, axis, keepdims=False)
        other = lax.dynamic_index_in_dim(x, 1 - core, axis, keepdims=False)
        return (kept.astype(f32) + swap(other).astype(f32)).astype(bf16)

    def over_shards(x):
        total = pieces_for(x, shard).astype(f32)
        for mask in range(1, shards):
            total = total + across(pieces_for(x, shard ^ mask), mask).astype(f32)
        return total

    in_rows = inproj_mean.shape[0]
    inproj_part = lax.dot_general(
        normed_all.reshape(flat, model_width), dproj, (((0,), (1,)), ((), ())), preferred_element_type=f32
    ).astype(bf16)
    inproj_part = over_cores(inproj_part.reshape(shards, places, 2, in_rows, -1), 2)
    inproj_part = over_shards(inproj_part).astype(bf16)
    received = in_order(
        [pieces_for(inproj_part, place)]
        + [along(pieces_for(inproj_part, (place + m) % places), -m) for m in range(1, places)]
    ).astype(f32)
    side = lambda lo, hi: received[:, :, lo:hi].transpose(1, 0, 2).reshape(in_rows, -1)
    at_shared = 2 * own_width
    inproj_grad = jnp.concatenate(
        [
            side(0, own_width),
            side(own_width, at_shared),
            jnp.sum(received[:, :, at_shared : at_shared + state_two], axis=0),
            side(at_shared + state_two, at_shared + state_two + heads),
        ],
        axis=1,
    )
    out_rows = outproj_mean.shape[0]
    outproj_part = jnp.dot(branch, cot_all.reshape(flat, model_width), preferred_element_type=f32).astype(bf16)
    outproj_part = over_cores(outproj_part.reshape(places, 2, out_rows, model_width), 1)
    outproj_part = over_shards(outproj_part)
    outproj_grad = lax.ppermute(
        outproj_part,
        ("wshard", "seq"),
        [
            (a * group + 2 * b + c, b * group + 2 * a + c)
            for a in range(shards)
            for b in range(places)
            for c in range(2)
        ],
    )

    conv_sums = jnp.sum(conv_acc, axis=-1)
    conv_part = jnp.concatenate(
        [
            lax.dynamic_update_slice_in_dim(
                jnp.zeros((kernel_len + 1, inner_width), f32),
                conv_sums[:, :own_width],
                place * own_width,
                1,
            ),
            conv_sums[:, own_width:],
        ],
        axis=1,
    )
    head_sums = jnp.sum(head_acc, axis=-1)[:, :heads]
    head_sums = jnp.concatenate([head_sums[:1] * rates, head_sums[1:]])
    head_part = lax.dynamic_update_slice_in_dim(
        jnp.zeros((3, head_count), f32), head_sums, place * heads, 1
    )
    sums = lax.psum(
        jnp.concatenate([conv_part.reshape(-1), head_part.reshape(-1)]), ("wshard", "seq")
    )
    conv_total = sums[: conv_part.size].reshape(conv_part.shape)
    head_total = sums[conv_part.size :].reshape(3, head_count)
    conv_width = conv_mean.shape[1]
    conv_grad = lax.dynamic_slice_in_dim(
        conv_total, (shard * group + seq_index) * conv_width, conv_width, 1
    )
    head_width = head_params.shape[1]
    head_grad = lax.dynamic_slice_in_dim(head_total, shard * head_width, head_width, 1)

    def own_piece(param, count, axis_dim):
        return lax.dynamic_slice_in_dim(param, seq_index * count, count, axis_dim).astype(f32)

    inproj_own = own_piece(inproj_weight, in_rows, 0)
    outproj_piece = own_piece(outproj_weight, out_rows, 0)
    norm_own = own_piece(norm_gain, in_rows, 0)
    gate_piece = own_piece(gate_gain, out_rows, 0)
    norm_grad = jnp.sum(inproj_own * inproj_grad, axis=1) / norm_own
    gate_grad = jnp.sum(outproj_piece * outproj_grad, axis=1) / gate_piece
    norm_res = adamw(norm_grad, norm_own, norm_mean, norm_square, 0.0)
    inproj_res = adamw(inproj_grad, inproj_own, inproj_mean, inproj_square, 0.1)
    conv_res = adamw(conv_grad, own_piece(conv_params, conv_width, 1), conv_mean, conv_square, 0.0)
    head_res = adamw(head_grad, head_params.astype(f32), head_mean, head_square, 0.0)
    gate_res = adamw(gate_grad, gate_piece, gate_mean, gate_square, 0.0)
    outproj_res = adamw(outproj_grad, outproj_piece, outproj_mean, outproj_square, 0.1)
    return (
        block_output,
        input_grad,
        norm_res[0],
        norm_res[1],
        norm_res[2],
        norm_res[3],
        inproj_res[0],
        inproj_res[1],
        inproj_res[2],
        inproj_res[3],
        conv_res[0],
        conv_res[1],
        conv_res[2],
        conv_res[3],
        head_res[0],
        head_res[1],
        head_res[2],
        head_res[3],
        gate_res[0],
        gate_res[1],
        gate_res[2],
        gate_res[3],
        outproj_res[0],
        outproj_res[1],
        outproj_res[2],
        outproj_res[3],
    )


def solution(mesh):
    placed = (
        P("wshard", "seq", None),
        P("wshard", "seq", None),
        P("wshard"),
        P(("wshard", "seq")),
        P(("wshard", "seq")),
        P("wshard", None),
        P(("wshard", "seq"), None),
        P(("wshard", "seq"), None),
        P(None, "wshard"),
        P(None, ("wshard", "seq")),
        P(None, ("wshard", "seq")),
        P(None, "wshard"),
        P(None, "wshard"),
        P(None, "wshard"),
        P("wshard"),
        P(("wshard", "seq")),
        P(("wshard", "seq")),
        P("wshard", None),
        P(("wshard", "seq"), None),
        P(("wshard", "seq"), None),
    )
    return jax.shard_map(
        local,
        mesh=mesh,
        in_specs=placed,
        out_specs=(
            P("wshard", "seq", None),
            P("wshard", "seq", None),
            P(("wshard", "seq")),
            P(("wshard", "seq")),
            P(("wshard", "seq")),
            P(("wshard", "seq")),
            P(("wshard", "seq"), None),
            P(("wshard", "seq"), None),
            P(("wshard", "seq"), None),
            P(("wshard", "seq"), None),
            P(None, ("wshard", "seq")),
            P(None, ("wshard", "seq")),
            P(None, ("wshard", "seq")),
            P(None, ("wshard", "seq")),
            P(None, "wshard"),
            P(None, "wshard"),
            P(None, "wshard"),
            P(None, "wshard"),
            P(("wshard", "seq")),
            P(("wshard", "seq")),
            P(("wshard", "seq")),
            P(("wshard", "seq")),
            P(("wshard", "seq"), None),
            P(("wshard", "seq"), None),
            P(("wshard", "seq"), None),
            P(("wshard", "seq"), None),
        ),
        check_vma=False,
    )
```

time: 1450 us -> 662 us (0.46)
  waiting for transfers between devices: 703 us -> 379 us
  local copies, waits for them, and re-layouts: 282 us -> 52.3 us
  matrix products: 174 us -> 28.6 us
  other arithmetic: 172 us -> 45.4 us
  Pallas kernels: 0 us -> 88.2 us
  blocking collectives: 72.7 us -> 0 us
  starting transfers between devices: 25.7 us -> 50.1 us
    reduce_scatter x2 -> x0, waiting for transfers between devices: 445 us -> none  [the longest x1 368 us: local(): lax.psum_scatter(grads[1], ('wshard', 'seq'), scatter_dimension=0, tiled=...]
    ppermute x0 -> x38, waiting for transfers between devices: none -> 260 us  [the longest x18 145 us: along(): lax.ppermute(x, 'seq', [(i, (i - 2 * step) % group) for i in range(group)])]
    unnamed x149 -> x78, local copies, waits for them, and re-layouts: 190 us -> 10.5 us
    all_gather x3 -> x1, waiting for transfers between devices: 178 us -> 0.01 us  [local(): outproj_all = lax.all_gather(outproj_weight, 'wshard', axis=0, tiled=True)]
    dot_general x21 -> x4, matrix products: 174 us -> 28.6 us  [the longest x1 11.3 us: local(): lax.dot_general(dproj, weight, (((0,), (0,)), ((), ())), preferred_elemen...]
    psum x0 -> x1, waiting for transfers between devices: none -> 119 us  [local(): lax.psum(jnp.concatenate([conv_part.reshape(-1), head_part.reshape(-1)]),...]
    pallas_call x0 -> x3, Pallas kernels: none -> 88.2 us  [the longest x1 44.1 us: run_backward(): pl.pallas_call(functools.partial(mixer_backward, own_width, heads, kernel...]
    all_to_all x6 -> x0, waiting for transfers between devices: 78.3 us -> none  [the longest x1 37.8 us: local(): lax.all_to_all(dsent.reshape(sequences, local_len, seq_devices, own_width...]
  transfers between devices with their start and end apart: 13 -> 40, of which waited for: 8 -> 15; matrix products, arithmetic and copies ran while one was open for 24% -> 14% of each run, Pallas kernels for 0% -> 5%
where the time goes in v1:
time: 662 us; the launch traced here: 659 us
  waiting for transfers between devices  379 us (57%)
  Pallas kernels  88.2 us (13%)
  local copies, waits for them, and re-layouts  52.3 us (8%)
  starting transfers between devices  50.1 us (8%)
  other arithmetic  45.4 us (7%)
  matrix products  28.6 us (4%)
  between operations  15.2 us (2%)
    ppermute x18, waiting for transfers between devices, along(): lax.ppermute(x, 'seq', [(i, (i - 2 * step) % group) for i in range(group)])  145 us
    psum x1, waiting for transfers between devices, local(): lax.psum(jnp.concatenate([conv_part.reshape(-1), head_part.reshape(-1)]),...  119 us
    ppermute x12, waiting for transfers between devices, across(): return lax.ppermute(x, 'wshard', [(i, i ^ mask) for i in range(shards)])  115 us
    pallas_call x1, Pallas kernels, run_backward(): pl.pallas_call(functools.partial(mixer_backward, own_width, heads, kernel...  44.1 us
    pallas_call x1, Pallas kernels, run_forward(): pl.pallas_call(functools.partial(mixer_forward, own_width, heads, kernel_...  35.4 us
    ppermute x18, starting transfers between devices, along(): lax.ppermute(x, 'seq', [(i, (i - 2 * step) % group) for i in range(group)])  28.9 us
    ppermute x12, starting transfers between devices, across(): return lax.ppermute(x, 'wshard', [(i, i ^ mask) for i in range(shards)])  19.5 us
  transfers between devices with their start and end apart: 40, of which 15 were waited for; matrix products, arithmetic and copies ran while one was open for 14% of the time, Pallas kernels for 5%

profile of v1, /device:TPU:0, one launch (start us, length us, event | category | flops | bytes accessed | tf_op | source)
XLA Modules:
  0.0 658.9 jit_solution(1211852567302996567)
XLA Ops:
  11.9 3.9 collective-permute-start.9
  16.6 1.5 collective-permute-start
  18.6 1.5 collective-permute-start.2
  21.6 49.7 %collective-permute-done = bf16[5348]{0:T(1024)(128)(2,1)S(1)} collective-permute-done((bf16[5348]{0:T(1024)(128)(2,1)S(1)}, bf16[5348]{0:T(1024)(128)(2,1)S(1)}, u32[]{:S(2)}, u32[]{:S(2)}) %collective-permute-start) | collective-permute-done | bytes 10728 | tf_op jit(solution)/shard_map/ppermute | solution.py:565
  74.5 1.4 reshape.288
  75.9 1.3 copy.101
  77.1 1.4 reshape.281
  80.0 14.9 %collective-permute-done.8 = bf16[912,384]{1,0:T(8,128)(2,1)} collective-permute-done((bf16[912,384]{1,0:T(8,128)(2,1)}, bf16[912,384]{1,0:T(8,128)(2,1)}, u32[]{:S(2)}, u32[]{:S(2)}) %collective-permute-start.8) | collective-permute-done | bytes 700448 | tf_op jit(solution)/shard_map/ppermute | solution.py:565
  94.9 1.7 pad_maximum_fusion.2
  97.1 1.9 fusion.29
  99.0 1.9 copy.114
  102.5 4.1 collective-permute-start.12
  109.6 3.1 collective-permute-start.4
  112.7 12.3 %collective-permute-done.12 = bf16[256,1536]{1,0:T(8,128)(2,1)} collective-permute-done((bf16[256,1536]{1,0:T(8,128)(2,1)}, bf16[256,1536]{1,0:T(8,128)(2,1)}, u32[]{:S(2)}, u32[]{:S(2)}) %collective-permute-start.12) | collective-permute-done | bytes 786464 | tf_op jit(solution)/shard_map/ppermute | solution.py:560
  126.1 48.8 %collective-permute-done.13 = bf16[256,1536]{1,0:T(8,128)(2,1)} collective-permute-done((bf16[256,1536]{1,0:T(8,128)(2,1)}, bf16[256,1536]{1,0:T(8,128)(2,1)}, u32[]{:S(2)}, u32[]{:S(2)}) %collective-permute-start.13) | collective-permute-done | bytes 786464 | tf_op jit(solution)/shard_map/ppermute | solution.py:560
  175.8 3.1 pad_maximum_fusion.1.cot_ref
  178.9 62.9 %collective-permute-done.5 = bf16[256,1536]{1,0:T(8,128)(2,1)S(1)} collective-permute-done((bf16[256,1536]{1,0:T(8,128)(2,1)S(1)}, bf16[256,1536]{1,0:T(8,128)(2,1)S(1)}, u32[]{:S(2)}, u32[]{:S(2)}) %collective-permute-start.5) | collective-permute-done | bytes 786464 | tf_op jit(solution)/shard_map/ppermute | solution.py:560
  241.8 1.9 pad_maximum_fusion.normed_ref
  243.7 3.0 broadcast_select_fusion
  247.1 2.4 copy-done.10
  249.5 35.4 %mixer_forward.1 = (f32[768,1024]{1,0:T(8,128)}, bf16[1024,1024]{1,0:T(8,128)(2,1)}, f32[1024,1024]{1,0:T(8,128)}, bf16[768,1024]{1,0:T(8,128)(2,1)}, f32[3,16,1...) custom-call(s32[4]{0:T(128)} %and_select_fusion.order_ref, bf16[4,256,1536]{2,1,0:T(8,128)(2,1)} %pad_maximum_fusion.normed_ref, ...), custom_call_target="tpu_custom_call" | custom-call | flops 11374952448 | bytes 25165824 | tf_op jit(solution)/shard_map/mixer_forward/pallas_call | solution.py:379
  284.9 3.2 constant_dynamic-slice_fusion.17.weight_ref
  288.1 8.8 %gate_statistics.1 = (f32[768,1024]{1,0:T(8,128)}, f32[8,1024]{1,0:T(8,128)}) custom-call(s32[4]{0:T(128)} %and_select_fusion.order_ref, f32[768,1024]{1,0:T(8,128)} %get-tuple-element.38.gates_ref, bf16[768,1024]{1,0:T(8,128)(2,1)} %get-tuple-element.39.sent_ref, bf16[4,256,1536]{2,1,0:T(8,128)(2,1)} %pad_maximum_fusion.1.cot_ref, ...), custom_call_target="tpu_custom_call" | custom-call | flops 2415919104 | bytes 16777216 | tf_op jit(solution)/shard_map/gate_statistics/pallas_call | solution.py:420
  297.7 3.0 collective-permute-start.16
  300.7 2.0 collective-permute-start.17
  302.7 2.5 constant_dynamic-slice_fusion.8
  308.1 44.1 %mixer_backward.1 = (bf16[1808,1024]{1,0:T(8,128)(2,1)}, bf16[768,1024]{1,0:T(8,128)(2,1)}, f32[5,1024,128]{2,1,0:T(8,128)}, f32[3,16,128]{2,1,0:T(8,128)}) custom-call(s32[4]{0:T(128)} %and_select_fusion.order_ref, f32[768,1024]{1,0:T(8,128)} %get-tuple-element.38.gates_ref, bf16[768,1024]{1,0:T(8,128)(2,1)} %get-tuple-element.39.sent_ref, ...), custom_call_target="tpu_custom_call" | custom-call | flops 17179869184 | bytes 33554432 | tf_op jit(solution)/shard_map/mixer_backward/pallas_call | solution.py:484
  353.7 1.6 slice_bitcast_fusion.2
  356.1 4.2 convolution_convert_fusion.2
  360.4 1.4 copy-done.7
  362.9 2.5 reduce_sum.67
  366.4 11.3 %convolution_convert_fusion.1 = bf16[1024,1536]{1,0:T(8,128)(2,1)} fusion(bf16[1808,1024]{1,0:T(8,128)(2,1)} %get-tuple-element.47, bf16[1808,1536]{1,0:T(8,128)(2,1)} %copy-done.10), kind=kOutput, calls=%fused_computation.5 | convolution fusion | flops 5689049088 | bytes 12402688 | tf_op jit(solution)/shard_map/dot_general | solution.py:696
  377.7 7.7 %convolution_convert_fusion = bf16[1536,1808]{0,1:T(8,128)(2,1)} fusion(bf16[1808,1024]{1,0:T(8,128)(2,1)S(1)} %copy-done.32, bf16[1024,1536]{1,0:T(8,128)(2,1)S(1)} %bitcast.125), kind=kOutput, calls=%fused_computation.2 | convolution fusion | flops 5690253312 | bytes 12402688 | tf_op jit(solution)/shard_map/dot_general | solution.py:721
  385.4 8.6 %copy.106 = bf16[1536,1808]{1,0:T(8,128)(2,1)} copy(bf16[1536,1808]{0,1:T(8,128)(2,1)} %convolution_convert_fusion) | data formatting | bytes 11108352 | tf_op jit(solution)/shard_map/convert_element_type | solution.py:723
  394.0 3.8 dynamic-slice_bitcast_fusion
  397.9 1.9 collective-permute-start.19
  399.8 2.2 collective-permute-start.20
  402.0 1.4 fusion.48
  404.0 1.4 collective-permute-start.23
  405.4 118.6 %all-reduce.6.cloned.1.call-done = f32[16784]{0:T(1024)} async-done(((f32[16784]{0:T(1024)}), f32[16784]{0:T(1024)}) %all-reduce.6.cloned.1.call-update) | async-done | bytes 67152 | tf_op jit(solution)/shard_map/psum | solution.py:774
  524.8 4.7 collective-permute-start.24
  531.1 1.4 add_multiply_fusion
  533.0 1.3 pad_maximum_fusion.4
  534.6 1.7 copy.104
  536.4 9.5 %collective-permute-done.24 = bf16[256,1536]{1,0:T(8,128)(2,1)} collective-permute-done((bf16[256,1536]{1,0:T(8,128)(2,1)}, bf16[256,1536]{1,0:T(8,128)(2,1)}, u32[]{:S(2)}, u32[]{:S(2)}) %collective-permute-start.24) | collective-permute-done | bytes 786464 | tf_op jit(solution)/shard_map/ppermute | solution.py:560
  545.9 2.2 convert_add_fusion.3
  548.3 1.4 copy-done.8
  549.8 1.7 fusion.3
  551.5 1.5 collective-permute-start.34
  555.1 5.3 fusion
  561.6 5.5 collective-permute-done.35
  568.3 2.5 fusion.2
  571.1 2.8 collective-permute-start.27
  573.8 5.3 collective-permute-start.28
  579.1 2.5 fusion.9
  581.7 2.6 fusion.24
  584.3 27.9 %collective-permute-done.27 = bf16[4,48,1808]{2,1,0:T(8,128)(2,1)S(1)} collective-permute-done((bf16[4,48,1808]{2,1,0:T(8,128)(2,1)S(1)}, bf16[4,48,1808]{2,1,0:T(8,128)(2,1)S(1)}, u32[]{:S(2)}, u32[]{:S(2)}) %collective-permute-start.27) | collective-permute-done | bytes 694304 | tf_op jit(solution)/shard_map/ppermute | solution.py:565
  612.2 7.0 %collective-permute-done.28 = bf16[4,48,1808]{2,1,0:T(8,128)(2,1)S(1)} collective-permute-done((bf16[4,48,1808]{2,1,0:T(8,128)(2,1)S(1)}, bf16[4,48,1808]{2,1,0:T(8,128)(2,1)S(1)}, u32[]{:S(2)}, u32[]{:S(2)}) %collective-permute-start.28) | collective-permute-done | bytes 694304 | tf_op jit(solution)/shard_map/ppermute | solution.py:565
  619.2 8.7 %collective-permute-done.29 = bf16[4,48,1808]{2,1,0:T(8,128)(2,1)S(1)} collective-permute-done((bf16[4,48,1808]{2,1,0:T(8,128)(2,1)S(1)}, bf16[4,48,1808]{2,1,0:T(8,128)(2,1)S(1)}, u32[]{:S(2)}, u32[]{:S(2)}) %collective-permute-start.29) | collective-permute-done | bytes 694304 | tf_op jit(solution)/shard_map/ppermute | solution.py:565
  628.5 3.6 collective-permute-start.31
  632.3 1.3 add_multiply_fusion.2
  633.6 4.3 collective-permute-done.30
  637.9 7.0 %collective-permute-done.31 = bf16[48,1808]{1,0:T(8,128)(2,1)S(1)} collective-permute-done((bf16[48,1808]{1,0:T(8,128)(2,1)S(1)}, bf16[48,1808]{1,0:T(8,128)(2,1)S(1)}, u32[]{:S(2)}, u32[]{:S(2)}) %collective-permute-start.31) | collective-permute-done | bytes 173600 | tf_op jit(solution)/shard_map/ppermute | solution.py:560
  645.7 4.2 fusion.19
  (226 shorter events, 39.5 us)
Async XLA Ops:
  7.2 277.7 %all-gather.2.cloned.1.call-start = ((), (), s32[]{:S(2)}) async-start(), calls=%async_computation | async-start | bytes 11796480 | tf_op jit(solution)/shard_map/all_gather | solution.py:669
  7.9 516.1 %all-reduce.6.cloned.1.call-start = ((), (), s32[]{:S(2)}) async-start(), calls=%async_computation.1 | async-start | bytes 139264 | tf_op jit(solution)/shard_map/psum | solution.py:774
  9.7 6.7 %copy-start.16 = (bf16[5,832]{1,0:T(8,128)(2,1)S(1)}, bf16[5,832]{1,0:T(8,128)(2,1)}, u32[]{:S(2)}) copy-start(bf16[5,832]{1,0:T(8,128)(2,1)} %param.28) | copy-start | bytes 24964
  9.7 6.8 %copy-start.25 = (bf16[3,12]{1,0:T(4,128)(2,1)S(1)}, bf16[3,12]{1,0:T(4,128)(2,1)}, u32[]{:S(2)}) copy-start(bf16[3,12]{1,0:T(4,128)(2,1)} %param.31) | copy-start | bytes 220
  9.7 6.8 %copy-start.20 = (bf16[768]{0:T(1024)(128)(2,1)S(1)}, bf16[768]{0:T(1024)(128)(2,1)}, u32[]{:S(2)}) copy-start(bf16[768]{0:T(1024)(128)(2,1)} %param.34) | copy-start | bytes 4612
  9.7 6.8 %copy-start.21 = (bf16[384]{0:T(512)(128)(2,1)S(1)}, bf16[384]{0:T(512)(128)(2,1)}, u32[]{:S(2)}) copy-start(bf16[384]{0:T(512)(128)(2,1)} %param.22) | copy-start | bytes 2308
  9.7 10.4 %copy-start.1 = (bf16[2,128,1536]{2,1,0:T(8,128)(2,1)S(1)}, bf16[2,128,1536]{2,1,0:T(8,128)(2,1)}, u32[]{:S(2)}) copy-start(bf16[2,128,1536]{2,1,0:T(8,128)(2,1)} %param.20) | copy-start | bytes 2359300
  10.9 9.4 %copy-start.5 = (bf16[2,128,1536]{2,1,0:T(8,128)(2,1)S(1)}, bf16[2,128,1536]{2,1,0:T(8,128)(2,1)}, u32[]{:S(2)}) copy-start(bf16[2,128,1536]{2,1,0:T(8,128)(2,1)} %param.21) | copy-start | bytes 2359300
  11.9 68.1 %collective-permute-start.9 = (bf16[912,384]{1,0:T(8,128)(2,1)}, bf16[912,384]{1,0:T(8,128)(2,1)}, u32[]{:S(2)}, u32[]{:S(2)}) collective-permute-start(bf16[912,384]{1,0:T(8,128)(2,1)} %get-tuple-element.122), channel_id=1, source_target_pairs={{0,24},{8,16},{16,8},{24,0},{1,25},{9,17},{17,9},{25,1},{2,26},{10... | collective-permute-start | bytes 2101256 | tf_op jit(solution)/shard_map/ppermute | solution.py:565
  15.8 64.2 %collective-permute-start.7 = (bf16[912,384]{1,0:T(8,128)(2,1)}, bf16[912,384]{1,0:T(8,128)(2,1)}, u32[]{:S(2)}, u32[]{:S(2)}) collective-permute-start(bf16[912,384]{1,0:T(8,128)(2,1)} %get-tuple-element.122), channel_id=1, source_target_pairs={{0,8},{8,0},{16,24},{24,16},{1,9},{9,1},{17,25},{25,17},{2,10},{10... | collective-permute-start | bytes 2101256 | tf_op jit(solution)/shard_map/ppermute | solution.py:565
  16.6 54.6 %collective-permute-start = (bf16[5348]{0:T(1024)(128)(2,1)S(1)}, bf16[5348]{0:T(1024)(128)(2,1)S(1)}, u32[]{:S(2)}, u32[]{:S(2)}) collective-permute-start(bf16[5348]{0:T(1024)(128)(2,1)S(1)} %concatenate.91), channel_id=1, source_target_pairs={{0,8},{8,0},{16,24},{24,16},{1,9},{9,1},{17,25},{25,17},{2,10},{10... | collective-permute-start | bytes 32096 | tf_op jit(solution)/shard_map/ppermute | solution.py:565
  18.1 53.2 %collective-permute-start.1 = (bf16[5348]{0:T(1024)(128)(2,1)S(1)}, bf16[5348]{0:T(1024)(128)(2,1)S(1)}, u32[]{:S(2)}, u32[]{:S(2)}) collective-permute-start(bf16[5348]{0:T(1024)(128)(2,1)S(1)} %concatenate.91), channel_id=1, source_target_pairs={{0,16},{8,24},{16,0},{24,8},{1,17},{9,25},{17,1},{25,9},{2,18},{10... | collective-permute-start | bytes 32096 | tf_op jit(solution)/shard_map/ppermute | solution.py:565
  18.6 53.0 %collective-permute-start.2 = (bf16[5348]{0:T(1024)(128)(2,1)S(1)}, bf16[5348]{0:T(1024)(128)(2,1)S(1)}, u32[]{:S(2)}, u32[]{:S(2)}) collective-permute-start(bf16[5348]{0:T(1024)(128)(2,1)S(1)} %concatenate.91), channel_id=1, source_target_pairs={{0,24},{8,16},{16,8},{24,0},{1,25},{9,17},{17,9},{25,1},{2,26},{10... | collective-permute-start | bytes 32096 | tf_op jit(solution)/shard_map/ppermute | solution.py:565
  71.3 23.7 %collective-permute-start.8 = (bf16[912,384]{1,0:T(8,128)(2,1)}, bf16[912,384]{1,0:T(8,128)(2,1)}, u32[]{:S(2)}, u32[]{:S(2)}) collective-permute-start(bf16[912,384]{1,0:T(8,128)(2,1)} %get-tuple-element.122), channel_id=1, source_target_pairs={{0,16},{8,24},{16,0},{24,8},{1,17},{9,25},{17,1},{25,9},{2,18},{10... | collective-permute-start | bytes 2101256 | tf_op jit(solution)/shard_map/ppermute | solution.py:565
  71.3 30.2 %collective-permute-start.11 = (bf16[128,1536]{1,0:T(8,128)(2,1)S(1)}, bf16[128,1536]{1,0:T(8,128)(2,1)S(1)}, u32[]{:S(2)}, u32[]{:S(2)}) collective-permute-start(bf16[128,1536]{1,0:T(8,128)(2,1)S(1)} %get-tuple-element.110), channel_id=1, source_target_pairs={{0,1},{1,0},{2,3},{3,2},{4,5},{5,4},{6,7},{7,6},{8,9},{9,8},{10,11... | collective-permute-start | bytes 1179656 | tf_op jit(solution)/shard_map/ppermute | solution.py:557
  73.6 35.8 %collective-permute-start.3 = (bf16[128,1536]{1,0:T(8,128)(2,1)}, bf16[128,1536]{1,0:T(8,128)(2,1)S(1)}, u32[]{:S(2)}, u32[]{:S(2)}) collective-permute-start(bf16[128,1536]{1,0:T(8,128)(2,1)} %get-tuple-element.112), channel_id=1, source_target_pairs={{0,1},{1,0},{2,3},{3,2},{4,5},{5,4},{6,7},{7,6},{8,9},{9,8},{10,11... | collective-permute-start | bytes 1179656 | tf_op jit(solution)/shard_map/ppermute | solution.py:557
  79.3 21.6 %copy-start.17 = (f32[3,12]{1,0:T(4,128)}, f32[3,12]{1,0:T(4,128)S(1)}, u32[]{:S(2)}) copy-start(f32[3,12]{1,0:T(4,128)S(1)} %constant_dynamic-slice_fusion.19) | copy-start | bytes 436
  100.9 5.8 copy-start.27
  100.9 142.8 %collective-permute-start.10 = (bf16[912,1536]{1,0:T(8,128)(2,1)}, bf16[912,1536]{1,0:T(8,128)(2,1)}, u32[]{:S(2)}, u32[]{:S(2)}) collective-permute-start(bf16[912,1536]{1,0:T(8,128)(2,1)} %bitcast.68), channel_id=1, source_target_pairs={{0,1},{1,0},{2,3},{3,2},{4,5},{5,4},{6,7},{7,6},{8,9},{9,8},{10,11... | collective-permute-start | bytes 8405000 | tf_op jit(solution)/shard_map/ppermute | solution.py:557
  102.5 22.4 %collective-permute-start.12 = (bf16[256,1536]{1,0:T(8,128)(2,1)}, bf16[256,1536]{1,0:T(8,128)(2,1)}, u32[]{:S(2)}, u32[]{:S(2)}) collective-permute-start(bf16[256,1536]{1,0:T(8,128)(2,1)} %maximum_select_fusion.5), channel_id=1, source_target_pairs={{0,6},{1,7},{2,0},{3,1},{4,2},{5,3},{6,4},{7,5},{8,14},{9,15},{10,... | collective-permute-start | bytes 2359304 | tf_op jit(solution)/shard_map/ppermute | solution.py:560
  106.7 68.2 %collective-permute-start.13 = (bf16[256,1536]{1,0:T(8,128)(2,1)}, bf16[256,1536]{1,0:T(8,128)(2,1)}, u32[]{:S(2)}, u32[]{:S(2)}) collective-permute-start(bf16[256,1536]{1,0:T(8,128)(2,1)} %maximum_select_fusion.5), channel_id=1, source_target_pairs={{0,4},{1,5},{2,6},{3,7},{4,0},{5,1},{6,2},{7,3},{8,12},{9,13},{10,... | collective-permute-start | bytes 2359304 | tf_op jit(solution)/shard_map/ppermute | solution.py:560
  108.4 67.4 %collective-permute-start.14 = (bf16[256,1536]{1,0:T(8,128)(2,1)}, bf16[256,1536]{1,0:T(8,128)(2,1)S(1)}, u32[]{:S(2)}, u32[]{:S(2)}) collective-permute-start(bf16[256,1536]{1,0:T(8,128)(2,1)} %maximum_select_fusion.5), channel_id=1, source_target_pairs={{0,2},{1,3},{2,4},{3,5},{4,6},{5,7},{6,0},{7,1},{8,10},{9,11},{10,... | collective-permute-start | bytes 2359304 | tf_op jit(solution)/shard_map/ppermute | solution.py:560
  109.6 69.3 %collective-permute-start.4 = (bf16[256,1536]{1,0:T(8,128)(2,1)S(1)}, bf16[256,1536]{1,0:T(8,128)(2,1)S(1)}, u32[]{:S(2)}, u32[]{:S(2)}) collective-permute-start(bf16[256,1536]{1,0:T(8,128)(2,1)S(1)} %maximum_select_fusion.3), channel_id=1, source_target_pairs={{0,6},{1,7},{2,0},{3,1},{4,2},{5,3},{6,4},{7,5},{8,14},{9,15},{10,... | collective-permute-start | bytes 2359304 | tf_op jit(solution)/shard_map/ppermute | solution.py:560
  124.9 116.9 %collective-permute-start.5 = (bf16[256,1536]{1,0:T(8,128)(2,1)S(1)}, bf16[256,1536]{1,0:T(8,128)(2,1)S(1)}, u32[]{:S(2)}, u32[]{:S(2)}) collective-permute-start(bf16[256,1536]{1,0:T(8,128)(2,1)S(1)} %maximum_select_fusion.3), channel_id=1, source_target_pairs={{0,4},{1,5},{2,6},{3,7},{4,0},{5,1},{6,2},{7,3},{8,12},{9,13},{10,... | collective-permute-start | bytes 2359304 | tf_op jit(solution)/shard_map/ppermute | solution.py:560
  174.8 67.0 %collective-permute-start.6 = (bf16[256,1536]{1,0:T(8,128)(2,1)S(1)}, bf16[256,1536]{1,0:T(8,128)(2,1)S(1)}, u32[]{:S(2)}, u32[]{:S(2)}) collective-permute-start(bf16[256,1536]{1,0:T(8,128)(2,1)S(1)} %maximum_select_fusion.3), channel_id=1, source_target_pairs={{0,2},{1,3},{2,4},{3,5},{4,6},{5,7},{6,0},{7,1},{8,10},{9,11},{10,... | collective-permute-start | bytes 2359304 | tf_op jit(solution)/shard_map/ppermute | solution.py:560
  297.7 9.0 %collective-permute-start.15 = (f32[2,1024]{1,0:T(2,128)S(1)}, f32[2,1024]{1,0:T(2,128)S(1)}, u32[]{:S(2)}, u32[]{:S(2)}) collective-permute-start(f32[2,1024]{1,0:T(2,128)S(1)} %slice.122), channel_id=1, source_target_pairs={{0,6},{1,7},{2,0},{3,1},{4,2},{5,3},{6,4},{7,5},{8,14},{9,15},{10,... | collective-permute-start | bytes 24584 | tf_op jit(solution)/shard_map/ppermute | solution.py:560
  297.7 9.0 %collective-permute-start.16 = (f32[2,1024]{1,0:T(2,128)S(1)}, f32[2,1024]{1,0:T(2,128)S(1)}, u32[]{:S(2)}, u32[]{:S(2)}) collective-permute-start(f32[2,1024]{1,0:T(2,128)S(1)} %slice.122), channel_id=1, source_target_pairs={{0,4},{1,5},{2,6},{3,7},{4,0},{5,1},{6,2},{7,3},{8,12},{9,13},{10,... | collective-permute-start | bytes 24584 | tf_op jit(solution)/shard_map/ppermute | solution.py:560
  300.7 6.0 collective-permute-start.17
  366.4 11.4 %copy-start.3 = (bf16[4,256,1536]{2,1,0:T(8,128)(2,1)S(1)}, bf16[4,256,1536]{2,1,0:T(8,128)(2,1)}, u32[]{:S(2)}) copy-start(bf16[4,256,1536]{2,1,0:T(8,128)(2,1)} %pad_maximum_fusion.normed_ref) | copy-start | bytes 9437188
  366.4 11.4 %copy-start.32 = (bf16[1808,1024]{1,0:T(8,128)(2,1)S(1)}, bf16[1808,1024]{1,0:T(8,128)(2,1)}, u32[]{:S(2)}) copy-start(bf16[1808,1024]{1,0:T(8,128)(2,1)} %get-tuple-element.47) | copy-start | bytes 11108356
  394.0 8.0 %copy-start.4 = (bf16[1024,1536]{1,0:T(8,128)(2,1)S(1)}, bf16[1024,1536]{1,0:T(8,128)(2,1)}, u32[]{:S(2)}) copy-start(bf16[1024,1536]{1,0:T(8,128)(2,1)} %convolution_convert_fusion.1) | copy-start | bytes 9437188
  397.8 127.0 %collective-permute-start.18 = (bf16[768,256]{1,0:T(8,128)(2,1)S(1)}, bf16[768,256]{1,0:T(8,128)(2,1)S(1)}, u32[]{:S(2)}, u32[]{:S(2)}) collective-permute-start(bf16[768,256]{1,0:T(8,128)(2,1)S(1)} %get-tuple-element.101), channel_id=1, source_target_pairs={{0,2},{1,3},{2,4},{3,5},{4,6},{5,7},{6,0},{7,1},{8,10},{9,11},{10,... | collective-permute-start | bytes 1179656 | tf_op jit(solution)/shard_map/ppermute | solution.py:560
  397.9 134.6 %collective-permute-start.19 = (bf16[768,256]{1,0:T(8,128)(2,1)S(1)}, bf16[768,256]{1,0:T(8,128)(2,1)}, u32[]{:S(2)}, u32[]{:S(2)}) collective-permute-start(bf16[768,256]{1,0:T(8,128)(2,1)S(1)} %get-tuple-element.100), channel_id=1, source_target_pairs={{0,4},{1,5},{2,6},{3,7},{4,0},{5,1},{6,2},{7,3},{8,12},{9,13},{10,... | collective-permute-start | bytes 1179656 | tf_op jit(solution)/shard_map/ppermute | solution.py:560
  399.8 129.7 %copy-start.23 = (f32[3,12]{1,0:T(4,128)S(1)}, f32[3,12]{1,0:T(4,128)}, u32[]{:S(2)}) copy-start(f32[3,12]{1,0:T(4,128)} %param.33) | copy-start | bytes 436
  399.8 129.7 %copy-start.24 = (f32[3,12]{1,0:T(4,128)S(1)}, f32[3,12]{1,0:T(4,128)}, u32[]{:S(2)}) copy-start(f32[3,12]{1,0:T(4,128)} %param.32) | copy-start | bytes 436
  399.8 129.7 %copy-start.26 = (bf16[3,12]{1,0:T(4,128)(2,1)S(1)}, bf16[3,12]{1,0:T(4,128)(2,1)}, u32[]{:S(2)}) copy-start(bf16[3,12]{1,0:T(4,128)(2,1)} %param.31) | copy-start | bytes 220
  399.8 131.3 %copy-start.18 = (f32[5,104]{1,0:T(8,128)S(1)}, f32[5,104]{1,0:T(8,128)}, u32[]{:S(2)}) copy-start(f32[5,104]{1,0:T(8,128)} %param.30) | copy-start | bytes 6244
  399.8 131.3 %copy-start.19 = (f32[5,104]{1,0:T(8,128)S(1)}, f32[5,104]{1,0:T(8,128)}, u32[]{:S(2)}) copy-start(f32[5,104]{1,0:T(8,128)} %param.29) | copy-start | bytes 6244
  399.8 132.7 %collective-permute-start.20 = (bf16[768,256]{1,0:T(8,128)(2,1)S(1)}, bf16[768,256]{1,0:T(8,128)(2,1)}, u32[]{:S(2)}, u32[]{:S(2)}) collective-permute-start(bf16[768,256]{1,0:T(8,128)(2,1)S(1)} %get-tuple-element.99), channel_id=1, source_target_pairs={{0,6},{1,7},{2,0},{3,1},{4,2},{5,3},{6,4},{7,5},{8,14},{9,15},{10,... | collective-permute-start | bytes 1179656 | tf_op jit(solution)/shard_map/ppermute | solution.py:560
  403.4 133.0 %collective-permute-start.22 = (bf16[256,1536]{1,0:T(8,128)(2,1)}, bf16[256,1536]{1,0:T(8,128)(2,1)}, u32[]{:S(2)}, u32[]{:S(2)}) collective-permute-start(bf16[256,1536]{1,0:T(8,128)(2,1)} %get-tuple-element.77), channel_id=1, source_target_pairs={{0,2},{1,3},{2,4},{3,5},{4,6},{5,7},{6,0},{7,1},{8,10},{9,11},{10,... | collective-permute-start | bytes 2359304 | tf_op jit(solution)/shard_map/ppermute | solution.py:560
  404.0 132.4 %collective-permute-start.23 = (bf16[256,1536]{1,0:T(8,128)(2,1)}, bf16[256,1536]{1,0:T(8,128)(2,1)}, u32[]{:S(2)}, u32[]{:S(2)}) collective-permute-start(bf16[256,1536]{1,0:T(8,128)(2,1)} %get-tuple-element.79), channel_id=1, source_target_pairs={{0,4},{1,5},{2,6},{3,7},{4,0},{5,1},{6,2},{7,3},{8,12},{9,13},{10,... | collective-permute-start | bytes 2359304 | tf_op jit(solution)/shard_map/ppermute | solution.py:560
  524.8 21.1 %collective-permute-start.24 = (bf16[256,1536]{1,0:T(8,128)(2,1)}, bf16[256,1536]{1,0:T(8,128)(2,1)}, u32[]{:S(2)}, u32[]{:S(2)}) collective-permute-start(bf16[256,1536]{1,0:T(8,128)(2,1)} %get-tuple-element.78), channel_id=1, source_target_pairs={{0,6},{1,7},{2,0},{3,1},{4,2},{5,3},{6,4},{7,5},{8,14},{9,15},{10,... | collective-permute-start | bytes 2359304 | tf_op jit(solution)/shard_map/ppermute | solution.py:560
  532.5 15.8 %collective-permute-start.33 = (bf16[4,96,1536]{2,1,0:T(8,128)(2,1)}, bf16[4,96,1536]{2,1,0:T(8,128)(2,1)}, u32[]{:S(2)}, u32[]{:S(2)}) collective-permute-start(bf16[4,96,1536]{2,1,0:T(8,128)(2,1)} %dynamic-slice_bitcast_fusion.1), channel_id=1, source_target_pairs={{0,1},{1,0},{2,3},{3,2},{4,5},{5,4},{6,7},{7,6},{8,9},{9,8},{10,11... | collective-permute-start | bytes 3538952 | tf_op jit(solution)/shard_map/ppermute | solution.py:557
  532.5 35.8 %collective-permute-start.26 = (bf16[4,4,48,1808]{3,2,1,0:T(8,128)(2,1)}, bf16[4,4,48,1808]{3,2,1,0:T(8,128)(2,1)}, u32[]{:S(2)}, u32[]{:S(2)}) collective-permute-start(bf16[4,4,48,1808]{3,2,1,0:T(8,128)(2,1)} %dynamic-slice_bitcast_fusion), channel_id=1, source_target_pairs={{0,1},{1,0},{2,3},{3,2},{4,5},{5,4},{6,7},{7,6},{8,9},{9,8},{10,11... | collective-permute-start | bytes 8331272 | tf_op jit(solution)/shard_map/ppermute | solution.py:557
  548.2 19.7 %collective-permute-start.25 = (f32[1,128,1536]{2,1,0:T(8,128)S(1)}, f32[1,128,1536]{2,1,0:T(8,128)S(1)}, u32[]{:S(2)}, u32[]{:S(2)}) collective-permute-start(f32[1,128,1536]{2,1,0:T(8,128)S(1)} %get-tuple-element.90), channel_id=1, source_target_pairs={{0,1},{1,0},{2,3},{3,2},{4,5},{5,4},{6,7},{7,6},{8,9},{9,8},{10,11... | collective-permute-start | bytes 2359304 | tf_op jit(solution)/shard_map/ppermute | solution.py:557
  549.8 5.3 copy-start.9
  551.4 16.9 %slice-start = ((s8[5898240]{0:T(1024)(128)(4,1)}), s8[4194304]{0:T(1024)(128)(4,1)S(1)}, s32[]{:S(2)}) async-start(s8[5898240]{0:T(1024)(128)(4,1)} %bitcast.117), calls=%async_computation.2 | async-start | bytes 8388608
  551.5 10.0 %collective-permute-start.34 = (bf16[96,1536]{1,0:T(8,128)(2,1)S(1)}, bf16[96,1536]{1,0:T(8,128)(2,1)S(1)}, u32[]{:S(2)}, u32[]{:S(2)}) collective-permute-start(bf16[96,1536]{1,0:T(8,128)(2,1)S(1)} %get-tuple-element.104), channel_id=1, source_target_pairs={{0,8},{8,0},{16,24},{24,16},{1,9},{9,1},{17,25},{25,17},{2,10},{10... | collective-permute-start | bytes 884744 | tf_op jit(solution)/shard_map/ppermute | solution.py:565
  553.1 14.0 %collective-permute-start.35 = (bf16[96,1536]{1,0:T(8,128)(2,1)S(1)}, bf16[96,1536]{1,0:T(8,128)(2,1)S(1)}, u32[]{:S(2)}, u32[]{:S(2)}) collective-permute-start(bf16[96,1536]{1,0:T(8,128)(2,1)S(1)} %get-tuple-element.106), channel_id=1, source_target_pairs={{0,16},{8,24},{16,0},{24,8},{1,17},{9,25},{17,1},{25,9},{2,18},{10... | collective-permute-start | bytes 884744 | tf_op jit(solution)/shard_map/ppermute | solution.py:565
  554.3 12.7 %collective-permute-start.36 = (bf16[96,1536]{1,0:T(8,128)(2,1)S(1)}, bf16[96,1536]{1,0:T(8,128)(2,1)S(1)}, u32[]{:S(2)}, u32[]{:S(2)}) collective-permute-start(bf16[96,1536]{1,0:T(8,128)(2,1)S(1)} %get-tuple-element.105), channel_id=1, source_target_pairs={{0,24},{8,16},{16,8},{24,0},{1,25},{9,17},{17,9},{25,1},{2,26},{10... | collective-permute-start | bytes 884744 | tf_op jit(solution)/shard_map/ppermute | solution.py:565
  555.1 13.2 %slice-start.1 = ((s8[5898240]{0:T(1024)(128)(4,1)}), s8[1703936]{0:T(1024)(128)(4,1)S(1)}, s32[]{:S(2)}) async-start(s8[5898240]{0:T(1024)(128)(4,1)} %bitcast.117), calls=%async_computation.3 | async-start | bytes 3407872
  560.6 7.4 %copy-start.15 = (f32[1536]{0:T(1024)S(1)}, f32[1536]{0:T(1024)}, u32[]{:S(2)}) copy-start(f32[1536]{0:T(1024)} %copy-done.14) | copy-start | bytes 18436
  561.5 17.6 %collective-permute-start.21 = (f32[1,128,1536]{2,1,0:T(8,128)S(1)}, f32[1,128,1536]{2,1,0:T(8,128)S(1)}, u32[]{:S(2)}, u32[]{:S(2)}) collective-permute-start(f32[1,128,1536]{2,1,0:T(8,128)S(1)} %get-tuple-element.93), channel_id=1, source_target_pairs={{0,1},{1,0},{2,3},{3,2},{4,5},{5,4},{6,7},{7,6},{8,9},{9,8},{10,11... | collective-permute-start | bytes 2359304 | tf_op jit(solution)/shard_map/ppermute | solution.py:557
  567.2 14.5 %collective-permute-start.37 = (f32[96,1536]{1,0:T(8,128)S(1)}, f32[96,1536]{1,0:T(8,128)S(1)}, u32[]{:S(2)}, u32[]{:S(2)}) collective-permute-start(f32[96,1536]{1,0:T(8,128)S(1)} %fusion.27), channel_id=1, source_target_pairs={{0,0},{1,1},{2,8},{3,9},{4,16},{5,17},{6,24},{7,25},{8,2},{9,3},{1... | collective-permute-start | bytes 1769480 | tf_op jit(solution)/shard_map/ppermute | solution.py:745
  570.9 8.2 %copy-start.6 = (bf16[2,128,1536]{2,1,0:T(8,128)(2,1)S(1)}, bf16[2,128,1536]{2,1,0:T(8,128)(2,1)}, u32[]{:S(2)}) copy-start(bf16[2,128,1536]{2,1,0:T(8,128)(2,1)} %param.21) | copy-start | bytes 2359300
  571.1 41.2 %collective-permute-start.27 = (bf16[4,48,1808]{2,1,0:T(8,128)(2,1)S(1)}, bf16[4,48,1808]{2,1,0:T(8,128)(2,1)S(1)}, u32[]{:S(2)}, u32[]{:S(2)}) collective-permute-start(bf16[4,48,1808]{2,1,0:T(8,128)(2,1)S(1)} %get-tuple-element.81), channel_id=1, source_target_pairs={{0,8},{8,0},{16,24},{24,16},{1,9},{9,1},{17,25},{25,17},{2,10},{10... | collective-permute-start | bytes 2082824 | tf_op jit(solution)/shard_map/ppermute | solution.py:565
  573.8 45.4 %collective-permute-start.28 = (bf16[4,48,1808]{2,1,0:T(8,128)(2,1)S(1)}, bf16[4,48,1808]{2,1,0:T(8,128)(2,1)S(1)}, u32[]{:S(2)}, u32[]{:S(2)}) collective-permute-start(bf16[4,48,1808]{2,1,0:T(8,128)(2,1)S(1)} %get-tuple-element.83), channel_id=1, source_target_pairs={{0,16},{8,24},{16,0},{24,8},{1,17},{9,25},{17,1},{25,9},{2,18},{10... | collective-permute-start | bytes 2082824 | tf_op jit(solution)/shard_map/ppermute | solution.py:565
  579.1 48.9 %collective-permute-start.29 = (bf16[4,48,1808]{2,1,0:T(8,128)(2,1)S(1)}, bf16[4,48,1808]{2,1,0:T(8,128)(2,1)S(1)}, u32[]{:S(2)}, u32[]{:S(2)}) collective-permute-start(bf16[4,48,1808]{2,1,0:T(8,128)(2,1)S(1)} %get-tuple-element.82), channel_id=1, source_target_pairs={{0,24},{8,16},{16,8},{24,0},{1,25},{9,17},{17,9},{25,1},{2,26},{10... | collective-permute-start | bytes 2082824 | tf_op jit(solution)/shard_map/ppermute | solution.py:565
  579.1 2.6 copy-start.11
  584.3 48.0 %copy-start.28 = (f32[96]{0:T(128)S(1)}, f32[96]{0:T(128)}, u32[]{:S(2)}) copy-start(f32[96]{0:T(128)} %param.36) | copy-start | bytes 1156
  584.3 48.0 %copy-start.29 = (f32[96]{0:T(128)S(1)}, f32[96]{0:T(128)}, u32[]{:S(2)}) copy-start(f32[96]{0:T(128)} %param.35) | copy-start | bytes 1156
  628.4 9.5 %collective-permute-start.30 = (bf16[48,1808]{1,0:T(8,128)(2,1)S(1)}, bf16[48,1808]{1,0:T(8,128)(2,1)S(1)}, u32[]{:S(2)}, u32[]{:S(2)}) collective-permute-start(bf16[48,1808]{1,0:T(8,128)(2,1)S(1)} %get-tuple-element.120), channel_id=1, source_target_pairs={{0,2},{1,3},{2,4},{3,5},{4,6},{5,7},{6,0},{7,1},{8,10},{9,11},{10,... | collective-permute-start | bytes 520712 | tf_op jit(solution)/shard_map/ppermute | solution.py:560
  628.5 16.5 %collective-permute-start.31 = (bf16[48,1808]{1,0:T(8,128)(2,1)S(1)}, bf16[48,1808]{1,0:T(8,128)(2,1)S(1)}, u32[]{:S(2)}, u32[]{:S(2)}) collective-permute-start(bf16[48,1808]{1,0:T(8,128)(2,1)S(1)} %get-tuple-element.119), channel_id=1, source_target_pairs={{0,4},{1,5},{2,6},{3,7},{4,0},{5,1},{6,2},{7,3},{8,12},{9,13},{10,... | collective-permute-start | bytes 520712 | tf_op jit(solution)/shard_map/ppermute | solution.py:560
  632.1 12.9 %collective-permute-start.32 = (bf16[48,1808]{1,0:T(8,128)(2,1)S(1)}, bf16[48,1808]{1,0:T(8,128)(2,1)S(1)}, u32[]{:S(2)}, u32[]{:S(2)}) collective-permute-start(bf16[48,1808]{1,0:T(8,128)(2,1)S(1)} %get-tuple-element.118), channel_id=1, source_target_pairs={{0,6},{1,7},{2,0},{3,1},{4,2},{5,3},{6,4},{7,5},{8,14},{9,15},{10,... | collective-permute-start | bytes 520712 | tf_op jit(solution)/shard_map/ppermute | solution.py:560
  (11 other events, 17.6 us)
Sparse Core Ops, SparseCore 0:
  9.9 126.6 all-gather.1
  366.5 157.4 all-reduce.5
